TPU v7x, 256 devices: a whole 4x4x8 slice. The times are simulated.
256 devices in a mesh: seg: 64 (over z_hi, x, y, core), row: 4 (over z_lo).
Axes of the slice: x: 4, y: 4, z: 8 (z_hi: 2, z_lo: 4; z = z_hi * 4 + z_lo), core: 2. Of those that a mesh axis runs over, the one named last changes fastest.
Arguments:
- fill_blocks: int32 [128, 4], P('seg'), may hold values from 0 to 7, all different within a row
- fill_mask: int32 [128, 4], P('seg'), may hold values 0 or 1
- inv_diag: float32 [128, 512, 512], P('seg'), as said below
- factor_off: float32 [128, 256, 512], P('seg', 'row'), may hold values from -1.4375 to 1.4375
Outputs:
- cov_diag: float32 [128, 512, 512], P('seg', 'row')
- cov_off: float32 [128, 256, 512], P('seg', 'row')
Inputs may be any that keep to these rules, and one draw needn't show every extreme that they name: The 4 entries of a row of fill_blocks are different. Each inv_diag[k] is lower triangular with a positive diagonal.
All inputs are finite; a program needn't handle non-finite values. No bound on the sum of `fill_mask` on one device may be relied on, other than what follows from the above.
Results may differ from a plain program's by a relative error of at most 0.0003.
Values sent between devices are 32-bit elements; how exact they have to be, the bound alone decides.
A program may use at most 64 MiB of HBM per device.

v0:
```python
import jax
import jax.numpy as jnp
from jax import lax
from jax.sharding import Mesh
from jax.sharding import PartitionSpec as P

BLOCK = 64
SEG = ("seg_0", "seg_1", "seg_2", "seg_3")


def laid_out(parts, dim):
    parts = jnp.moveaxis(parts, 0, dim)
    dims = parts.shape
    return parts.reshape(*dims[:dim], dims[dim] * dims[dim + 1], *dims[dim + 2 :])


def sent_to_all(value, axis):
    devices = lax.axis_size(axis)
    return lax.all_to_all(
        jnp.broadcast_to(value[None], (devices, *value.shape)), axis, 0, 0, tiled=True
    )


def collect(value, axis, dim):
    return laid_out(sent_to_all(value, axis), dim)


def from_behind(block, axis, distance):
    devices = range(lax.axis_size(axis))
    route = [(i - distance, i) for i in devices if i - distance in devices]
    return lax.ppermute(block, axis, route)


def neutral_like(value, identity):
    return jax.tree.map(
        lambda part, zero: jnp.zeros_like(part) + jnp.asarray(zero, part.dtype), value, identity
    )


def entering(value, axes, combine, identity):
    before = start = neutral_like(value, identity)
    so_far = value
    for axis in reversed(axes):
        devices, place = (lax.axis_size(axis), lax.axis_index(axis))
        pieces = jax.tree.map(lambda part: lax.all_gather(part, axis), so_far)
        inside, so_far = (start, start)
        for k in reversed(range(devices)):
            passed = k > place
            so_far = combine(so_far, jax.tree.map(lambda part: part[k], pieces))
            inside = jax.tree.map(lambda new, old: jnp.where(passed, new, old), so_far, inside)
        before = combine(inside, before)
    return before


def product(left, right):
    return jnp.dot(left, right, precision=lax.Precision.HIGHEST, preferred_element_type=jnp.float32)


def pick_columns(matrix, chosen_blocks):
    col_blocks = matrix.shape[1] // BLOCK
    tiles = jnp.take(matrix.reshape(matrix.shape[0], col_blocks, BLOCK), chosen_blocks, axis=1)
    return tiles.reshape(matrix.shape[0], chosen_blocks.shape[0] * BLOCK)


def body(fill_blocks, fill_mask, inv_diag, factor_off):
    panels = inv_diag.shape[0]
    panel_width = inv_diag.shape[2]
    seg_count = lax.axis_size(SEG)
    row_count = lax.axis_size("row")
    seg_at = lax.axis_index(SEG)
    row_at = lax.axis_index("row")
    local_rows = factor_off.shape[1]
    slots_here = local_rows // BLOCK
    cols_here = panel_width // row_count
    slot_live = fill_mask.astype(jnp.float32)
    global_panel = seg_at * panels + jnp.arange(panels, dtype=jnp.int32)
    not_last = (global_panel < seg_count * panels - 1).astype(jnp.float32)
    live_here = lax.dynamic_slice_in_dim(slot_live, row_at * slots_here, slots_here, 1)
    row_keep = jnp.repeat(live_here * not_last[:, None], BLOCK, axis=1)
    slot_keep = jnp.repeat(live_here, BLOCK, axis=1)
    local_map = jnp.einsum(
        "prw,pwv->prv",
        factor_off * row_keep[:, :, None],
        inv_diag,
        precision=lax.Precision.HIGHEST,
        preferred_element_type=jnp.float32,
    )
    factor_map = collect(local_map, "row", 1)
    prior_fill = from_behind(fill_blocks[panels - 1 :], SEG, 1)
    before_fill = jnp.concatenate([prior_fill, fill_blocks[: panels - 1]], 0)
    link_maps = []
    base_terms = []
    for position in range(panels):
        link_maps.append(pick_columns(factor_map[position], before_fill[position]))
        chosen = pick_columns(inv_diag[position], before_fill[position])
        base_terms.append(product(chosen.T, chosen))
    carried = link_maps[panels - 1]
    constant = base_terms[panels - 1]
    position = 0
    constant = (
        product(link_maps[position].T, product(constant, link_maps[position]))
        + base_terms[position]
    )
    carried = product(carried, link_maps[position])
    nothing = jnp.zeros_like(constant)

    def compose(earlier, later):
        return (
            product(earlier[0], later[0]),
            product(later[0].T, product(earlier[1], later[0])) + later[1],
        )

    identity = jnp.eye(carried.shape[0], dtype=jnp.float32)
    incoming_cov = entering((carried, constant), SEG, compose, (identity, nothing))[1]
    diag_parts = [None] * panels
    cross_parts = [None] * panels
    for position in range(panels - 1, -1, -1):
        weighted = product(incoming_cov, factor_map[position])
        own_rows = lax.dynamic_slice_in_dim(weighted, row_at * local_rows, local_rows, 0)
        cross_parts[position] = -own_rows * slot_keep[position][:, None]
        inverse_cols = lax.dynamic_slice_in_dim(
            inv_diag[position], row_at * cols_here, cols_here, 1
        )
        factor_cols = lax.dynamic_slice_in_dim(
            factor_map[position], row_at * cols_here, cols_here, 1
        )
        diag_parts[position] = product(inverse_cols.T, inv_diag[position]) + product(
            factor_cols.T, weighted
        )
        incoming_cov = (
            product(link_maps[position].T, product(incoming_cov, link_maps[position]))
            + base_terms[position]
        )
    return (jnp.stack(diag_parts), jnp.stack(cross_parts))


def solution(mesh):
    torus = Mesh(
        mesh.devices.reshape(2, 4, 4, 2, mesh.shape["row"]),
        ("seg_0", "seg_1", "seg_2", "seg_3", "row"),
    )
    placed = (P(SEG, None), P(SEG, None), P(SEG, None, None), P(SEG, "row", None))
    return jax.shard_map(
        body,
        mesh=torus,
        in_specs=placed,
        out_specs=(P(SEG, "row", None), P(SEG, "row", None)),
        check_vma=False,
    )
```

profile of v0, /device:TPU:32, one launch (start us, length us, event | category | flops | bytes accessed | tf_op | source)
XLA Modules:
  0.0 218.0 jit_solution(12386908197665848362)
XLA Ops:
  7.2 0.7 slice.114
  7.8 1.7 collective-permute-start
  9.6 0.7 convert_element_type.12
  10.5 3.1 %fusion.41 = f32[2,64,512]{2,1,0:T(8,128)S(1)} fusion(f32[2,512,512]{2,1,0:T(8,128)} %param.10, f32[2,64,512]{2,1,0:T(8,128)} %param.11, f32[2]{0:T(128)S(1)} %get-tuple-element.6), kind=kOutput, calls=%fused_computation.71 | convolution fusion | flops 402718720 | bytes 2621448 | tf_op jit(solution)/shard_map/prw,pwv->prv/dot_general | solution.py:81
  13.6 1.1 broadcast_in_dim.28
  14.7 6.0 %all-to-all-start = ((f32[4,2,64,512]{3,2,1,0:T(8,128)}), f32[4,2,64,512]{3,2,1,0:T(8,128)}, u32[]{:S(2)}, u32[]{:S(2)}) async-start(f32[4,2,64,512]{3,2,1,0:T(8,128)} %broadcast_in_dim.28), calls=%async_computation | async-start | bytes 2097152 | tf_op jit(solution)/shard_map/all_to_all | solution.py:19
  20.7 1.5 fusion.129
  22.2 2.5 %copy.14 = f32[1,512,512]{1,2,0:T(8,128)} copy(f32[1,512,512]{2,1,0:T(8,128)} %get-tuple-element.8) | data formatting | bytes 2097152
  24.8 2.6 %copy.15 = f32[1,512,512]{1,2,0:T(8,128)} copy(f32[1,512,512]{2,1,0:T(8,128)} %get-tuple-element.9) | data formatting | bytes 2097152
  27.3 1.8 gather_fusion.2
  29.3 1.3 fusion.133
  30.6 2.4 %fusion.7 = f32[128,512]{1,0:T(8,128)} fusion(f32[1,512,512]{1,2,0:T(8,128)} %copy.14, s32[]{:T(128)S(6)} %select_n.140, f32[2,512,512]{2,1,0:T(8,128)S(1)} %copy-done), kind=kOutput, calls=%fused_computation.28 | convolution fusion | flops 402653184 | bytes 1572868 | tf_op jit(solution)/shard_map/dot_general | solution.py:56
  33.0 1.8 gather_fusion.3
  34.8 0.9 broadcast_select_fusion
  35.7 8.2 %all-to-all-done = f32[4,2,64,512]{3,2,1,0:T(8,128)} async-done(((f32[4,2,64,512]{3,2,1,0:T(8,128)}), f32[4,2,64,512]{3,2,1,0:T(8,128)}, u32[]{:S(2)}, u32[]{:S(2)}) %all-to-all-start) | async-done | bytes 1048608 | tf_op jit(solution)/shard_map/all_to_all | solution.py:19
  44.0 1.3 fusion.130
  45.3 1.2 reshape_squeeze.13
  46.4 2.3 %copy.12 = f32[256,8,64]{0,2,1:T(8,128)} copy(f32[256,8,64]{2,1,0:T(8,128)} %reshape_squeeze.13) | data formatting | bytes 1048576 | tf_op jit(solution)/shard_map/reshape;squeeze | solution.py:61
  48.8 1.6 gather_fusion.1
  50.4 0.8 broadcast_select_fusion.2
  51.2 1.2 reshape_squeeze.12
  52.4 2.3 %copy.11 = f32[256,8,64]{0,2,1:T(8,128)} copy(f32[256,8,64]{2,1,0:T(8,128)} %reshape_squeeze.12) | data formatting | bytes 1048576 | tf_op jit(solution)/shard_map/reshape;squeeze | solution.py:61
  54.7 1.6 gather_fusion
  57.0 2.5 %all-gather = f32[512,256]{1,0:T(8,128)S(1)} all-gather(f32[256,256]{1,0:T(8,128)S(1)} %fusion.132), channel_id=2, replica_groups=mesh['seg_0'=2,'seg_1'=4,'seg_2'=4,'seg_3'=2,'row'=4] {'seg_3'}, dimensions={0}, use_global_device_ids=true | all-gather | bytes 786432 | tf_op jit(solution)/shard_map/all_gather | solution.py:45
  59.9 0.7 copy-done.8
  60.6 1.1 fusion.84
  61.7 1.9 fusion.135
  63.6 1.4 fusion.134
  65.5 2.2 %all-gather.4 = f32[512,256]{1,0:T(8,128)S(1)} all-gather(f32[256,256]{1,0:T(8,128)S(1)} %convolution_add_fusion.12), channel_id=6, replica_groups=mesh['seg_0'=2,'seg_1'=4,'seg_2'=4,'seg_3'=2,'row'=4] {'seg_3'}, dimensions={0}, use_global_device_ids=true | all-gather | bytes 786432 | tf_op jit(solution)/shard_map/all_gather | solution.py:45
  68.3 0.7 copy-done.9
  69.3 1.3 convolution_add_fusion.11
  70.9 2.4 %fusion.5 = f32[128,512]{1,0:T(8,128)} fusion(f32[1,512,512]{1,2,0:T(8,128)} %copy.15, s32[]{:T(128)S(6)} %select_n.140, f32[2,512,512]{2,1,0:T(8,128)S(1)} %copy-done), kind=kOutput, calls=%fused_computation.26 | convolution fusion | flops 402653184 | bytes 1572868 | tf_op jit(solution)/shard_map/dot_general | solution.py:56
  73.8 1.2 fusion.20
  75.1 1.0 fusion.25
  76.1 16.9 %all-gather.13.cloned.1.call-done = f32[1024,256]{1,0:T(8,128)} async-done(((f32[256,256]{1,0:T(8,128)}), f32[1024,256]{1,0:T(8,128)}) %all-gather.13.cloned.1.call-update) | async-done | bytes 1048592 | tf_op jit(solution)/shard_map/all_gather | solution.py:45
  92.9 1.3 fusion.39
  94.3 1.3 fusion.77
  95.6 1.3 fusion.72
  97.0 1.1 fusion.67
  98.2 23.6 %all-gather.17.cloned.1.call-done = f32[1024,256]{1,0:T(8,128)} async-done(((f32[256,256]{1,0:T(8,128)}), f32[1024,256]{1,0:T(8,128)}) %all-gather.17.cloned.1.call-update) | async-done | bytes 1048592 | tf_op jit(solution)/shard_map/all_gather | solution.py:45
  121.8 1.6 convolution_add_fusion.14
  123.8 1.5 convolution_add_fusion.10
  125.4 0.7 copy-done.14
  126.5 0.6 convolution_add_fusion.9
  127.1 0.7 copy-done.15
  128.2 1.3 convolution_add_fusion.8
  130.0 1.5 fusion.28
  131.5 1.3 fusion.139
  132.8 18.4 %all-gather.15.cloned.1.call-done = f32[1024,256]{1,0:T(8,128)} async-done(((f32[256,256]{1,0:T(8,128)}), f32[1024,256]{1,0:T(8,128)}) %all-gather.15.cloned.1.call-update) | async-done | bytes 1048592 | tf_op jit(solution)/shard_map/all_gather | solution.py:45
  151.2 1.1 multiply_reduce_fusion.2
  152.3 1.2 fusion.38
  153.6 1.3 fusion.60
  154.9 1.3 fusion.55
  156.6 16.1 %all-gather.3 = f32[512,256]{1,0:T(8,128)S(1)} all-gather(f32[256,256]{1,0:T(8,128)S(1)} %fusion.50), channel_id=5, replica_groups=mesh['seg_0'=2,'seg_1'=4,'seg_2'=4,'seg_3'=2,'row'=4] {'seg_0'}, dimensions={0}, use_global_device_ids=true | all-gather | bytes 786432 | tf_op jit(solution)/shard_map/all_gather | solution.py:45
  173.2 6.7 %all-gather.19.cloned.1.call-done = f32[1024,256]{1,0:T(8,128)} async-done(((f32[256,256]{1,0:T(8,128)}), f32[1024,256]{1,0:T(8,128)}) %all-gather.19.cloned.1.call-update) | async-done | bytes 1048592 | tf_op jit(solution)/shard_map/all_gather | solution.py:45
  179.9 1.6 convolution_add_fusion.15
  182.0 1.5 convolution_add_fusion.7
  185.9 15.9 %all-gather.7 = f32[512,256]{1,0:T(8,128)S(1)} all-gather(f32[256,256]{1,0:T(8,128)S(1)} %convolution_add_fusion.5), channel_id=9, replica_groups=mesh['seg_0'=2,'seg_1'=4,'seg_2'=4,'seg_3'=2,'row'=4] {'seg_0'}, dimensions={0}, use_global_device_ids=true | all-gather | bytes 786432 | tf_op jit(solution)/shard_map/all_gather | solution.py:45
  203.5 0.6 fusion.4
  206.3 0.6 fusion.142
  207.0 0.6 fusion.141
  208.6 1.3 multiply_bitcast_fusion
  209.9 0.7 pad_maximum_fusion.1
  210.6 0.8 pad_maximum_fusion
  (90 shorter events, 13.5 us)
Async XLA Ops:
  7.8 25.1 %collective-permute-start = (s32[1,4]{1,0:T(1,128)S(1)}, s32[1,4]{1,0:T(1,128)S(1)}, u32[]{:S(2)}, u32[]{:S(2)}) collective-permute-start(s32[1,4]{1,0:T(1,128)S(1)} %slice.114), channel_id=1, source_target_pairs={{0,4},{4,8},{8,12},{12,16},{16,20},{20,24},{24,28},{28,32},{32,36}... | collective-permute-start | bytes 56 | tf_op jit(solution)/shard_map/ppermute | solution.py:31
  13.6 7.1 %copy-start.22 = (s32[2,4]{1,0:T(2,128)S(1)}, s32[2,4]{1,0:T(2,128)}, u32[]{:S(2)}) copy-start(s32[2,4]{1,0:T(2,128)} %param.8) | copy-start | bytes 100
  13.6 7.1 %copy-start = (f32[2,512,512]{2,1,0:T(8,128)S(1)}, f32[2,512,512]{2,1,0:T(8,128)}, u32[]{:S(2)}) copy-start(f32[2,512,512]{2,1,0:T(8,128)} %param.10) | copy-start | bytes 6291460
  14.7 29.3 %all-to-all-start = ((f32[4,2,64,512]{3,2,1,0:T(8,128)}), f32[4,2,64,512]{3,2,1,0:T(8,128)}, u32[]{:S(2)}, u32[]{:S(2)}) async-start(f32[4,2,64,512]{3,2,1,0:T(8,128)} %broadcast_in_dim.28), calls=%async_computation | async-start | bytes 2097152 | tf_op jit(solution)/shard_map/all_to_all | solution.py:19
  20.7 72.2 %all-gather.13.cloned.1.call-start = ((), (), s32[]{:S(2)}) async-start(), calls=%async_computation.1 | async-start | bytes 1310720 | tf_op jit(solution)/shard_map/all_gather | solution.py:45
  45.3 5.1 %copy-start.3 = (f32[1,4,64,512]{3,2,0,1:T(8,128)}, f32[1,4,64,512]{3,2,0,1:T(8,128)S(1)}, u32[]{:S(2)}) copy-start(f32[1,4,64,512]{3,2,0,1:T(8,128)S(1)} %get-tuple-element.10) | copy-start | bytes 1572868
  51.2 5.2 %copy-start.5 = (f32[4,256,64]{1,2,0:T(8,128)S(1)}, f32[4,256,64]{1,2,0:T(8,128)}, u32[]{:S(2)}) copy-start(f32[4,256,64]{1,2,0:T(8,128)} %broadcast_select_fusion.2) | copy-start | bytes 786436
  59.9 0.7 copy-start.8
  61.7 60.1 %all-gather.17.cloned.1.call-start = ((), (), s32[]{:S(2)}) async-start(), calls=%async_computation.3 | async-start | bytes 1310720 | tf_op jit(solution)/shard_map/all_gather | solution.py:45
  61.7 3.4 %copy-start.6 = (f32[4,256,64]{1,2,0:T(8,128)S(1)}, f32[4,256,64]{1,2,0:T(8,128)}, u32[]{:S(2)}) copy-start(f32[4,256,64]{1,2,0:T(8,128)} %broadcast_select_fusion.2) | copy-start | bytes 786436
  68.3 0.7 copy-start.9
  70.6 4.4 %copy-start.10 = (f32[256,256]{1,0:T(8,128)S(1)}, f32[256,256]{1,0:T(8,128)}, u32[]{:S(2)}) copy-start(f32[256,256]{1,0:T(8,128)} %copy-done.9) | copy-start | bytes 786436
  70.6 4.4 %copy-start.13 = (f32[256,256]{1,0:T(8,128)S(1)}, f32[256,256]{1,0:T(8,128)}, u32[]{:S(2)}) copy-start(f32[256,256]{1,0:T(8,128)} %convolution_add_fusion.11) | copy-start | bytes 786436
  70.7 80.5 %all-gather.15.cloned.1.call-start = ((), (), s32[]{:S(2)}) async-start(), calls=%async_computation.2 | async-start | bytes 1310720 | tf_op jit(solution)/shard_map/all_gather | solution.py:45
  92.9 4.0 %copy-start.1 = (f32[1024,256]{1,0:T(8,128)S(1)}, f32[1024,256]{1,0:T(8,128)}, u32[]{:S(2)}) copy-start(f32[1024,256]{1,0:T(8,128)} %all-gather.13.cloned.1.call-done) | copy-start | bytes 3145732
  98.1 81.9 %all-gather.19.cloned.1.call-start = ((), (), s32[]{:S(2)}) async-start(), calls=%async_computation.4 | async-start | bytes 1310720 | tf_op jit(solution)/shard_map/all_gather | solution.py:45
  121.8 4.7 %copy-start.18 = (f32[1024,256]{1,0:T(8,128)S(1)}, f32[1024,256]{1,0:T(8,128)}, u32[]{:S(2)}) copy-start(f32[1024,256]{1,0:T(8,128)} %all-gather.17.cloned.1.call-done) | copy-start | bytes 3145732
  123.5 4.8 %copy-start.12 = (f32[256,256]{1,0:T(8,128)}, f32[256,256]{1,0:T(8,128)S(1)}, u32[]{:S(2)}) copy-start(f32[256,256]{1,0:T(8,128)S(1)} %convolution_add_fusion.14) | copy-start | bytes 786436
  125.4 0.7 copy-start.14
  126.1 3.4 %copy-start.11 = (f32[256,256]{1,0:T(8,128)S(1)}, f32[256,256]{1,0:T(8,128)}, u32[]{:S(2)}) copy-start(f32[256,256]{1,0:T(8,128)} %fusion.67) | copy-start | bytes 786436
  127.1 0.7 copy-start.15
  151.2 5.0 %copy-start.2 = (f32[1024,256]{1,0:T(8,128)S(1)}, f32[1024,256]{1,0:T(8,128)}, u32[]{:S(2)}) copy-start(f32[1024,256]{1,0:T(8,128)} %all-gather.15.cloned.1.call-done) | copy-start | bytes 3145732
  179.9 4.0 %copy-start.19 = (f32[1024,256]{1,0:T(8,128)S(1)}, f32[1024,256]{1,0:T(8,128)}, u32[]{:S(2)}) copy-start(f32[1024,256]{1,0:T(8,128)} %all-gather.19.cloned.1.call-done) | copy-start | bytes 3145732
  202.5 2.6 %copy-start.16 = (f32[256,256]{1,0:T(8,128)S(1)}, f32[256,256]{1,0:T(8,128)}, u32[]{:S(2)}) copy-start(f32[256,256]{1,0:T(8,128)} %fusion.139) | copy-start | bytes 786436
  202.5 2.6 %copy-start.17 = (f32[256,256]{1,0:T(8,128)S(1)}, f32[256,256]{1,0:T(8,128)}, u32[]{:S(2)}) copy-start(f32[256,256]{1,0:T(8,128)} %fusion.25) | copy-start | bytes 786436
  204.1 1.8 copy-start.7
  205.2 1.8 copy-start.4
  205.5 2.1 copy-start.20
  206.3 1.8 copy-start.21
Sparse Core Ops, SparseCore 0:
  61.8 31.1 all-gather.12
  94.7 27.0 all-gather.16
  124.2 26.9 all-gather.14
  152.9 27.0 all-gather.18
where the time goes:
time: 219 us; the launch traced here: 218 us
  waiting for transfers between devices  73.9 us (34%)
  matrix products  50.9 us (23%)
  blocking collectives  36.8 us (17%)
  local copies, waits for them, and re-layouts  26.9 us (12%)
  between operations  14.5 us (7%)
  starting transfers between devices  8.04 us (4%)
  other arithmetic  6.91 us (3%)
    all_gather x4, waiting for transfers between devices, entering(): pieces = jax.tree.map(lambda part: lax.all_gather(part, axis), so_far)  65.6 us
    dot_general x54, matrix products, product(): jnp.dot(left, right, precision=lax.Precision.HIGHEST, preferred_element_t...  47.8 us
    all_gather x4, blocking collectives, entering(): pieces = jax.tree.map(lambda part: lax.all_gather(part, axis), so_far)  36.8 us
    all_to_all x1, waiting for transfers between devices, sent_to_all(): lax.all_to_all(jnp.broadcast_to(value[None], (devices, *value.shape)), ax...  8.24 us
    unnamed x48, local copies, waits for them, and re-layouts  7.92 us
    another operation x4, local copies, waits for them, and re-layouts, pick_columns(): matrix.reshape(matrix.shape[0], col_blocks, BLOCK)  7.01 us
    gather x4, local copies, waits for them, and re-layouts, pick_columns(): jnp.take(matrix.reshape(matrix.shape[0], col_blocks, BLOCK), chosen_block...  6.81 us
    all_to_all x1, starting transfers between devices, sent_to_all(): lax.all_to_all(jnp.broadcast_to(value[None], (devices, *value.shape)), ax...  6 us
  transfers between devices with their start and end apart: 6, of which 5 were waited for; matrix products, arithmetic and copies ran while one was open for 24% of the time, Pallas kernels for 0%

commit v1 on v0

v1 whole, which is shorter than its diff:
```python
import jax
import jax.numpy as jnp
from jax import lax
from jax.experimental import pallas as pl
from jax.experimental.pallas import tpu as pltpu
from jax.sharding import Mesh
from jax.sharding import PartitionSpec as P

BLOCK = 64
SEG = ("seg_0", "seg_1", "seg_2", "seg_3")
F32 = jnp.float32
BF16 = jnp.bfloat16
N_IDS = 100

ID_IDX = 0
ID_ZL = 1
ID_ZF = 13
ID_CL = 25
ID_CA = 26
ID_YL = 27
ID_YA = 39
ID_XL = 51
ID_XA = 63
ID_ZH = 75


def split(v):
    hi = v.astype(BF16)
    return hi, (v - hi.astype(F32)).astype(BF16)


def dot(a, b):
    return lax.dot_general(a, b, (((1,), (0,)), ((), ())), preferred_element_type=F32)


def mm(a, b):
    (ah, al), (bh, bl) = a, b
    return dot(ah, bh) + (dot(ah, bl) + dot(al, bh))


def sandwich(link, inner, added):
    left = mm(split(link.T), split(inner))
    return added + mm(split(left), split(link))


def kernel(
    blocks, mask, inv, fac, cov, off,
    idx_out, idx_in, inv_h, inv_l, lp, fg, base, cl, ca, yl, ya, xl, xa,
    el, ea, ph, th, pb, ss, rs,
):
    h, x, y, c = (lax.axis_index(a) for a in SEG)
    r = lax.axis_index("row")
    z = 4 * h + r
    seg = ((h * 4 + x) * 4 + y) * 2 + c

    def z_at(d):
        zz = lax.rem(z + d + 8, 8)
        return {"seg_0": zz // 4, "row": lax.rem(zz, 4)}

    def seg_at(d):
        s = lax.rem(seg + d + 64, 64)
        return {
            "seg_0": s // 32,
            "seg_1": lax.rem(s // 8, 4),
            "seg_2": lax.rem(s // 2, 4),
            "seg_3": lax.rem(s, 2),
        }

    def y_at(d):
        return {"seg_2": lax.rem(y + d + 4, 4)}

    def x_at(d):
        return {"seg_1": lax.rem(x + d + 4, 4)}

    mate = {"seg_3": 1 - c}

    barrier = pltpu.get_barrier_semaphore()
    greeted = (mate, z_at(1), z_at(-1), y_at(1), y_at(-1), x_at(1), x_at(-1), seg_at(1), seg_at(-1))
    for who in greeted:
        pl.semaphore_signal(barrier, 1, device_id=who, device_id_type=pl.DeviceIdType.MESH)

    started = []

    def copy(src, dst, number, who):
        return pltpu.make_async_remote_copy(
            src_ref=src, dst_ref=dst, send_sem=ss.at[number], recv_sem=rs.at[number],
            device_id=who, device_id_type=pl.DeviceIdType.MESH,
        )

    lane = lax.broadcasted_iota(jnp.int32, (8, 256), 1)
    slot = lane // BLOCK

    def targets(panel):
        t = jnp.zeros((8, 256), jnp.int32)
        for s in range(4):
            t = jnp.where(slot == s, blocks[panel, s], t)
        return t * BLOCK + (lane - slot * BLOCK)

    idx_out[...] = targets(1)
    target_1 = targets(0)

    row_at = lax.broadcasted_iota(jnp.int32, (512, 256), 0)

    def chooser(t):
        return jnp.where(row_at == t[0:1, :], 1.0, 0.0).astype(BF16)

    def keep(panel):
        live = mask[panel, r].astype(F32)
        return jnp.where(seg * 2 + panel < 127, live, 0.0)

    frows = [None, None]
    for p in (1, 0):
        ih, il = split(inv[p])
        inv_h[p] = ih
        inv_l[p] = il
        frows[p] = mm(split(fac[p] * keep(p)), (ih, il))
        fg[p, pl.ds(r * 64, 64), :] = frows[p]

    def local_link(p, choose):
        fh, fl = split(fg[p, pl.ds(r * 64, 64), :])
        lp[p, pl.ds(r * 64, 64), :] = dot(fh, choose) + dot(fl, choose)

    def local_base(p, choose):
        ch = dot(inv_h[p], choose)
        cl_ = dot(inv_l[p], choose)
        chh, cll = ch.astype(BF16), cl_.astype(BF16)
        cth, ctl = ch.T.astype(BF16), cl_.T.astype(BF16)
        base[p] = mm((cth, ctl), (chh, cll))

    choose_1 = chooser(target_1)
    local_link(1, choose_1)

    pl.semaphore_wait(barrier, 9)

    idx_copy = copy(idx_out, idx_in, ID_IDX, seg_at(1))
    idx_copy.start()
    started.append((None, idx_copy))

    def z_parts(buf, ids, p, k, up):
        block = (r - k) if up else (r + k)
        block_in = (r - 1 - k) if up else (r + 1 + k)
        sends = jnp.logical_and(r < 3, r - k >= 0) if up else jnp.logical_and(r > 0, r + k <= 3)
        takes = (r - 1 - k >= 0) if up else (r + 1 + k <= 3)
        number = ids + p * 6 + (0 if up else 3) + k
        who = z_at(1 if up else -1)

        def made(b):
            part = buf.at[p, pl.ds(b * 64, 64), :]
            return copy(part, part, number, who)

        return sends, takes, lambda: made(block), lambda: made(block_in)

    def z_send(buf, ids, p, k):
        for up in (True, False):
            sends, _, out, _ = z_parts(buf, ids, p, k, up)

            @pl.when(sends)
            def _():
                out().start()

            started.append((sends, out))

    def z_take(buf, ids, p, k):
        for up in (True, False):
            _, takes, _, into = z_parts(buf, ids, p, k, up)

            @pl.when(takes)
            def _():
                into().wait_recv()

    z_send(lp, ID_ZL, 1, 0)
    idx_copy.wait_recv()
    choose_0 = chooser(idx_in[...])
    local_link(0, choose_0)
    z_send(lp, ID_ZL, 0, 0)
    local_base(1, choose_1)
    local_base(0, choose_0)
    for k in range(3):
        for p in (1, 0):
            z_take(lp, ID_ZL, p, k)
            if k < 2:
                z_send(lp, ID_ZL, p, k + 1)
    for p in (1, 0):
        z_send(fg, ID_ZF, p, 0)

    link_0 = split(lp[0])
    cl[c] = mm(split(lp[1]), link_0)
    cl_copy = copy(cl.at[c], cl.at[c], ID_CL, mate)
    cl_copy.start()
    ca[c] = sandwich(lp[0], base[1], base[0])
    ca_copy = copy(ca.at[c], ca.at[c], ID_CA, mate)
    ca_copy.start()
    started.append((None, cl_copy))
    started.append((None, ca_copy))

    def half(j):
        return pl.ds(c * 128 + j * 64, 64)

    def ring_send(buf, ids, at, where):
        for step, (way, j) in enumerate(((0, 0), (1, 1), (0, 1), (1, 0))):
            part = buf.at[at, half(j), :]
            one = copy(part, part, ids + way * 2 + j, where(1 if way == 0 else -1))
            one.start()
            started.append((None, one))

    def ring_pass(buf, ids, at, where):
        def mated(place, j, number):
            part = buf.at[place, half(j), :]
            one = copy(part, part, number, mate)
            one.start()
            started.append((None, one))
            return one

        mates = []
        behind, ahead, across = (lax.rem(at + d, 4) for d in (3, 1, 2))
        for way, j in ((0, 0), (1, 1), (0, 1), (1, 0)):
            place = behind if way == 0 else ahead
            part = buf.at[place, half(j), :]
            copy(part, part, ids + way * 2 + j, where(1)).wait_recv()
            if way == j:
                onward = copy(part, part, ids + 4 + way, where(1 if way == 0 else -1))
                onward.start()
                started.append((None, onward))
            mates.append(mated(place, j, ids + 6 + way * 2 + j))
        for way in (0, 1):
            part = buf.at[across, half(way), :]
            copy(part, part, ids + 4 + way, where(1)).wait_recv()
            mates.append(mated(across, way, ids + 10 + way))
        for one in mates:
            one.wait_recv()

    def scan_links(buf, at, own, out):
        eye = lax.broadcasted_iota(jnp.int32, (256, 256), 0) == lax.broadcasted_iota(jnp.int32, (256, 256), 1)

        @pl.when(at == 3)
        def _():
            own[...] = eye.astype(F32)

        total = buf[3]
        for i in (2, 1, 0):

            @pl.when(at == i)
            def _():
                own[...] = total

            total = mm(split(total), split(buf[i]))
        if out is not None:
            out[0][out[1]] = total

    def scan_constants(links, buf, at, own):
        @pl.when(at == 3)
        def _():
            own[...] = jnp.zeros((256, 256), F32)

        total = buf[3]
        for i in (2, 1, 0):

            @pl.when(at == i)
            def _():
                own[...] = total

            total = sandwich(links[i], total, buf[i])
        return total

    cl_copy.wait_recv()
    yl[y] = mm(split(cl[1]), split(cl[0]))
    ring_send(yl, ID_YL, y, y_at)
    ca_copy.wait_recv()
    ya[y] = sandwich(cl[0], ca[1], ca[0])
    ring_send(ya, ID_YA, y, y_at)

    for p in (0, 1):
        mine = inv[p, :, pl.ds(pl.multiple_of(r * 128, 128), 128)]
        cov[p] = mm(split(mine.T), (inv_h[p], inv_l[p]))

    ring_pass(yl, ID_YL, y, y_at)
    scan_links(yl, y, el.at[0], (xl, x))
    ring_send(xl, ID_XL, x, x_at)
    for p in (1, 0):
        z_take(fg, ID_ZF, p, 0)
        z_send(fg, ID_ZF, p, 1)
    ring_pass(ya, ID_YA, y, y_at)
    xa[x] = scan_constants(yl, ya, y, ea.at[0])
    ring_send(xa, ID_XA, x, x_at)

    ring_pass(xl, ID_XL, x, x_at)
    scan_links(xl, x, el.at[1], None)
    for p in (1, 0):
        z_take(fg, ID_ZF, p, 1)
        z_send(fg, ID_ZF, p, 2)
    ring_pass(xa, ID_XA, x, x_at)
    th[...] = scan_constants(xl, xa, x, ea.at[1])

    edge = jnp.logical_or(r == 0, r == 3)
    hop = z_at(jnp.where(r == 0, -1, 1))
    inward = z_at(jnp.where(r == 0, 1, -1))

    def zh(j, kind):
        part = ph.at[half(j), :]
        if kind == 0:
            return copy(th.at[half(j), :], part, ID_ZH + j, hop)
        if kind == 1:
            return copy(part, part, ID_ZH + 2 + j, inward)
        return copy(part, part, ID_ZH + 4 + j, mate)

    later = h == 1

    @pl.when(jnp.logical_and(later, edge))
    def _():
        for j in (0, 1):
            zh(j, 0).start()

    link = mm(split(el[1]), split(el[0]))
    constant = sandwich(el[0], ea[1], ea[0])
    el[2] = link
    ea[2] = constant

    @pl.when(c == 0)
    def _():
        el[2] = mm(split(link), split(cl[1]))
        ea[2] = sandwich(cl[1], constant, ca[1])

    for p in (1, 0):
        z_take(fg, ID_ZF, p, 2)

    @pl.when(later)
    def _():
        pb[1] = ea[2]

    @pl.when(jnp.logical_and(h == 0, edge))
    def _():
        for j in (0, 1):
            zh(j, 0).wait_recv()
            zh(j, 1).start()
            zh(j, 2).start()

    @pl.when(jnp.logical_and(h == 0, jnp.logical_not(edge)))
    def _():
        for j in (0, 1):
            zh(j, 1).wait_recv()
            zh(j, 2).start()

    @pl.when(h == 0)
    def _():
        for j in (0, 1):
            zh(j, 2).wait_recv()
        pb[1] = sandwich(el[2], ph[...], ea[2])

    pb[0] = sandwich(lp[1], pb[1], base[1])

    for p in (1, 0):
        full = split(fg[p])
        mine = fg[p, :, pl.ds(pl.multiple_of(r * 128, 128), 128)]
        middle = mm(split(pb[p]), split(mine))
        cov[p] += mm(split(middle.T), full)
        rows = mm(split(pb[p, pl.ds(r * 64, 64), :]), full)
        off[p] = rows * (-mask[p, r].astype(F32))

    for sends, one in started:
        if sends is None:
            one.wait_send()
        else:

            @pl.when(sends)
            def _():
                one().wait_send()

    @pl.when(jnp.logical_and(later, edge))
    def _():
        for j in (0, 1):
            zh(j, 0).wait_send()

    @pl.when(jnp.logical_and(h == 0, edge))
    def _():
        for j in (0, 1):
            zh(j, 1).wait_send()

    @pl.when(h == 0)
    def _():
        for j in (0, 1):
            zh(j, 2).wait_send()


def body(fill_blocks, fill_mask, inv_diag, factor_off):
    vmem = pl.BlockSpec(memory_space=pltpu.VMEM)
    smem = pl.BlockSpec(memory_space=pltpu.SMEM)

    def sq(n):
        return pltpu.VMEM((n, 256, 256), F32)

    return pl.pallas_call(
        kernel,
        name="chain",
        out_shape=(
            jax.ShapeDtypeStruct((2, 128, 512), F32),
            jax.ShapeDtypeStruct((2, 64, 512), F32),
        ),
        in_specs=[smem, smem, vmem, vmem],
        out_specs=(vmem, vmem),
        scratch_shapes=[
            pltpu.VMEM((8, 256), jnp.int32),
            pltpu.VMEM((8, 256), jnp.int32),
            pltpu.VMEM((2, 512, 512), BF16),
            pltpu.VMEM((2, 512, 512), BF16),
            sq(2),
            pltpu.VMEM((2, 256, 512), F32),
            sq(2),
            sq(2),
            sq(2),
            sq(4),
            sq(4),
            sq(4),
            sq(4),
            sq(3),
            sq(3),
            pltpu.VMEM((256, 256), F32),
            pltpu.VMEM((256, 256), F32),
            sq(2),
            pltpu.SemaphoreType.DMA((N_IDS,)),
            pltpu.SemaphoreType.DMA((N_IDS,)),
        ],
        compiler_params=pltpu.CompilerParams(
            collective_id=0, has_side_effects=True, vmem_limit_bytes=48 << 20
        ),
    )(fill_blocks, fill_mask, inv_diag, factor_off)


def solution(mesh):
    torus = Mesh(mesh.devices.reshape(2, 4, 4, 2, mesh.shape["row"]), (*SEG, "row"))
    placed = (P(SEG, None), P(SEG, None), P(SEG, None, None), P(SEG, "row", None))
    return jax.shard_map(
        body,
        mesh=torus,
        in_specs=placed,
        out_specs=(P(SEG, "row", None), P(SEG, "row", None)),
        check_vma=False,
    )
```

time: 219 us -> 83.4 us (0.38)
  the two profiles are of different devices: /device:TPU:32 before, /device:TPU:33 now
where the time goes in v1:
time: 83.4 us; the launch traced here: 83.2 us
  Pallas kernels  77.2 us (93%)
  local copies, waits for them, and re-layouts  5.39 us (6%)
    pallas_call x1, Pallas kernels, body(): pl.pallas_call(kernel, name='chain', out_shape=(jax.ShapeDtypeStruct((2,...  77.2 us
    unnamed x10, local copies, waits for them, and re-layouts  5.39 us

profile of v1, /device:TPU:33, one launch (start us, length us, event | category | flops | bytes accessed | tf_op | source)
XLA Modules:
  0.0 83.2 jit_solution(12447261564781419472)
XLA Ops:
  0.6 0.0 copy-start
  0.6 1.6 %copy-done = f32[2,512,512]{2,1,0:T(8,128)S(1)} copy-done((f32[2,512,512]{2,1,0:T(8,128)S(1)}, f32[2,512,512]{2,1,0:T(8,128)}, u32[]{:S(2)}) %copy-start) | copy-done | bytes 2097176
  2.2 0.0 copy-start.1
  2.2 0.9 %copy-done.1 = f32[2,64,512]{2,1,0:T(8,128)S(1)} copy-done((f32[2,64,512]{2,1,0:T(8,128)S(1)}, f32[2,64,512]{2,1,0:T(8,128)}, u32[]{:S(2)}) %copy-start.1) | copy-done | bytes 262168
  3.2 0.0 copy-start.2
  3.2 0.7 copy-done.2
  3.9 0.0 copy-start.3
  3.9 0.7 copy-done.3
  4.5 77.2 %chain.1 = (f32[2,128,512]{2,1,0:T(8,128)S(1)}, f32[2,64,512]{2,1,0:T(8,128)S(1)}) custom-call(s32[2,4]{1,0:T(2,128)S(1)} %copy-done.2, s32[2,4]{1,0:T(2,128)S(1)} %copy-done.3, f32[2,512,512]{2,1,0:T(8,128)S(1)} %copy-done, f32[2,64,512]{2,1,0:T(8,128)S(1)} %copy-done.1), custom_call_target="tpu_custom_call" | custom-call | tf_op jit(solution)/shard_map/chain/pallas_call | solution.py:391
  81.7 0.8 copy.8
  82.5 0.7 copy.9
Async XLA Ops:
  0.6 1.6 %copy-start = (f32[2,512,512]{2,1,0:T(8,128)S(1)}, f32[2,512,512]{2,1,0:T(8,128)}, u32[]{:S(2)}) copy-start(f32[2,512,512]{2,1,0:T(8,128)} %inv.1) | copy-start | bytes 6291460
  2.2 0.9 %copy-start.1 = (f32[2,64,512]{2,1,0:T(8,128)S(1)}, f32[2,64,512]{2,1,0:T(8,128)}, u32[]{:S(2)}) copy-start(f32[2,64,512]{2,1,0:T(8,128)} %fac.1) | copy-start | bytes 786436
  3.2 0.7 copy-start.2
  3.9 0.7 copy-start.3

commit v2 on v1

v2 whole, which is shorter than its diff:
```python
import jax
import jax.numpy as jnp
from jax import lax
from jax.experimental import pallas as pl
from jax.experimental.pallas import tpu as pltpu
from jax.sharding import Mesh
from jax.sharding import PartitionSpec as P

BLOCK = 64
SEG = ("seg_0", "seg_1", "seg_2", "seg_3")
F32 = jnp.float32
BF16 = jnp.bfloat16
N_IDS = 100

ID_IDX = 0
ID_ZL = 1
ID_ZF = 13
ID_CL = 25
ID_CA = 26
ID_YL = 27
ID_YA = 39
ID_XL = 51
ID_XA = 63
ID_RELAY = 99
ID_ZH = 75


def split(v):
    hi = v.astype(BF16)
    return hi, (v - hi.astype(F32)).astype(BF16)


def dot(a, b):
    return lax.dot_general(a, b, (((1,), (0,)), ((), ())), preferred_element_type=F32)


def mm(a, b):
    (ah, al), (bh, bl) = a, b
    return dot(ah, bh) + (dot(ah, bl) + dot(al, bh))


def sandwich(link, inner, added):
    left = mm(split(link.T), split(inner))
    return added + mm(split(left), split(link))


def kernel(
    blocks_hbm, mask_hbm, inv_hbm, fac_hbm, cov, off,
    blocks, mask, inv, fac, local, idx_out, idx_in, inv_h, inv_l, lp, fg, base, cl, ca, yl, ya, xl, xa,
    el, ea, ph, th, pb, rb, gg, kk, ss, rs,
):
    h, x, y, c = (lax.axis_index(a) for a in SEG)
    r = lax.axis_index("row")
    z = 4 * h + r
    seg = ((h * 4 + x) * 4 + y) * 2 + c

    def z_at(d):
        zz = lax.rem(z + d + 8, 8)
        return {"seg_0": zz // 4, "row": lax.rem(zz, 4)}

    def seg_at(d):
        s = lax.rem(seg + d + 64, 64)
        return {
            "seg_0": s // 32,
            "seg_1": lax.rem(s // 8, 4),
            "seg_2": lax.rem(s // 2, 4),
            "seg_3": lax.rem(s, 2),
        }

    def y_at(d):
        return {"seg_2": lax.rem(y + d + 4, 4)}

    def x_at(d):
        return {"seg_1": lax.rem(x + d + 4, 4)}

    mate = {"seg_3": 1 - c}

    barrier = pltpu.get_barrier_semaphore()

    def greet(who):
        pl.semaphore_signal(barrier, 1, device_id=who, device_id_type=pl.DeviceIdType.MESH)

    for who in (mate, z_at(1), z_at(-1), y_at(1), y_at(-1), x_at(1), x_at(-1)):
        greet(who)

    both = jnp.logical_and
    later = h == 1
    edge = jnp.logical_or(r == 0, r == 3)
    tail = both(both(x == 3, y == 3), c == 1)
    head = both(both(x == 0, y == 0), c == 0)
    plain_out, plain_in = jnp.logical_not(tail), jnp.logical_not(head)
    far_out = both(both(tail, h == 0), edge)
    far_in = both(both(head, later), edge)
    relay_in = both(both(head, later), jnp.logical_not(edge))
    across_half = {
        "seg_0": 1 - h, "seg_1": lax.rem(x + 1 + 2 * h, 4), "seg_2": lax.rem(y + 1 + 2 * h, 4),
        "seg_3": 1 - c, "row": 3 - r,
    }
    for cond, who in (
        (plain_out, seg_at(1)), (plain_in, seg_at(-1)), (far_out, across_half), (far_in, across_half),
    ):

        @pl.when(cond)
        def _():
            greet(who)

    greetings = 7
    for cond in (plain_out, plain_in, far_out, far_in):
        greetings = greetings + jnp.where(cond, 1, 0)

    loads = [
        pltpu.make_async_copy(src, dst, local.at[i])
        for i, (src, dst) in enumerate((
            (blocks_hbm, blocks), (mask_hbm, mask), (fac_hbm, fac),
            (inv_hbm.at[1], inv.at[1]), (inv_hbm.at[0], inv.at[0]),
        ))
    ]
    for load in loads:
        load.start()

    started = []

    def copy(src, dst, number, who):
        return pltpu.make_async_remote_copy(
            src_ref=src, dst_ref=dst, send_sem=ss.at[number], recv_sem=rs.at[number],
            device_id=who, device_id_type=pl.DeviceIdType.MESH,
        )

    for load in loads[:3]:
        load.wait()

    lane = lax.broadcasted_iota(jnp.int32, (8, 256), 1)
    slot = lane // BLOCK

    def targets(panel):
        t = jnp.zeros((8, 256), jnp.int32)
        for s in range(4):
            t = jnp.where(slot == s, blocks[panel, s], t)
        return t * BLOCK + (lane - slot * BLOCK)

    idx_out[...] = targets(1)
    target_1 = targets(0)

    row_at = lax.broadcasted_iota(jnp.int32, (512, 256), 0)

    def chooser(t):
        return jnp.where(row_at == t[0:1, :], 1.0, 0.0).astype(BF16)

    def keep(panel):
        live = mask[panel, r].astype(F32)
        return jnp.where(seg * 2 + panel < 127, live, 0.0)

    frows = [None, None]
    for p in (1, 0):
        loads[4 - p].wait()
        ih, il = split(inv[p])
        inv_h[p] = ih
        inv_l[p] = il
        frows[p] = mm(split(fac[p] * keep(p)), (ih, il))
        fg[p, pl.ds(r * 64, 64), :] = frows[p]

    def local_link(p, choose):
        fh, fl = split(fg[p, pl.ds(r * 64, 64), :])
        lp[p, pl.ds(r * 64, 64), :] = dot(fh, choose) + dot(fl, choose)

    def local_base(p, choose):
        ch = dot(inv_h[p], choose)
        cl_ = dot(inv_l[p], choose)
        chh, cll = ch.astype(BF16), cl_.astype(BF16)
        cth, ctl = ch.T.astype(BF16), cl_.T.astype(BF16)
        base[p] = mm((cth, ctl), (chh, cll))

    choose_1 = chooser(target_1)
    local_link(1, choose_1)

    pl.semaphore_wait(barrier, greetings)

    def begin(cond, made):
        @pl.when(cond)
        def _():
            made().start()

        started.append((cond, made))

    begin(plain_out, lambda: copy(idx_out, idx_in, ID_IDX, seg_at(1)))
    begin(far_out, lambda: copy(idx_out, idx_in, ID_IDX, across_half))
    inward = z_at(jnp.where(r == 0, 1, -1))
    relay = lambda: copy(idx_in, idx_in, ID_RELAY, inward)

    def z_parts(buf, ids, p, k, up):
        block = (r - k) if up else (r + k)
        block_in = (r - 1 - k) if up else (r + 1 + k)
        sends = jnp.logical_and(r < 3, r - k >= 0) if up else jnp.logical_and(r > 0, r + k <= 3)
        takes = (r - 1 - k >= 0) if up else (r + 1 + k <= 3)
        number = ids + p * 6 + (0 if up else 3) + k
        who = z_at(1 if up else -1)

        def made(b):
            part = buf.at[p, pl.ds(b * 64, 64), :]
            return copy(part, part, number, who)

        return sends, takes, lambda: made(block), lambda: made(block_in)

    def z_send(buf, ids, p, k):
        for up in (True, False):
            sends, _, out, _ = z_parts(buf, ids, p, k, up)

            @pl.when(sends)
            def _():
                out().start()

            started.append((sends, out))

    def z_take(buf, ids, p, k):
        for up in (True, False):
            _, takes, _, into = z_parts(buf, ids, p, k, up)

            @pl.when(takes)
            def _():
                into().wait_recv()

    z_send(lp, ID_ZL, 1, 0)
    local_base(1, choose_1)

    @pl.when(jnp.logical_or(plain_in, far_in))
    def _():
        copy(idx_out, idx_in, ID_IDX, mate).wait_recv()

    begin(far_in, relay)

    @pl.when(relay_in)
    def _():
        relay().wait_recv()

    @pl.when(both(head, h == 0))
    def _():
        idx_in[...] = target_1

    choose_0 = chooser(idx_in[...])
    local_link(0, choose_0)
    z_send(lp, ID_ZL, 0, 0)
    local_base(0, choose_0)
    for k in range(3):
        for p in (1, 0):
            z_take(lp, ID_ZL, p, k)
            if k < 2:
                z_send(lp, ID_ZL, p, k + 1)
        if k == 0:
            for p in (0, 1):
                mine = inv[p, :, pl.ds(pl.multiple_of(r * 128, 128), 128)]
                cov[p] = mm(split(mine.T), (inv_h[p], inv_l[p]))
    for p in (1, 0):
        z_send(fg, ID_ZF, p, 0)

    link_0 = split(lp[0])
    cl[c] = mm(split(lp[1]), link_0)
    cl_copy = copy(cl.at[c], cl.at[c], ID_CL, mate)
    cl_copy.start()
    ca[c] = sandwich(lp[0], base[1], base[0])
    ca_copy = copy(ca.at[c], ca.at[c], ID_CA, mate)
    ca_copy.start()
    started.append((None, cl_copy))
    started.append((None, ca_copy))

    turn = 1 - 2 * c

    def link_part(j):
        return pl.ds(c * 128 + j * 64, 64), slice(None)

    def constant_part(j):
        if j == 0:
            at = pl.ds(pl.multiple_of(c * 128, 128), 128)
            return at, at
        return pl.ds(c * 64, 64), pl.ds(128, 128)

    def ring_send(buf, ids, at, where, part):
        for way, j in ((0, 0), (1, 1), (0, 1), (1, 0)):
            piece = buf.at[at, *part(j)]
            one = copy(piece, piece, ids + way * 2 + j, where(turn if way == 0 else -turn))
            one.start()
            started.append((None, one))

    def places(at):
        return tuple(lax.rem(at + d + 4, 4) for d in (-turn, turn, 2))

    def mated(buf, place, j, number, part):
        piece = buf.at[place, *part(j)]
        one = copy(piece, piece, number, mate)
        one.start()
        started.append((None, one))
        return one

    def ring_pass(buf, ids, at, where, part):
        behind, ahead, across = places(at)
        mates = []
        for way, j in ((0, 0), (1, 1), (0, 1), (1, 0)):
            place = behind if way == 0 else ahead
            piece = buf.at[place, *part(j)]
            copy(piece, piece, ids + way * 2 + j, mate).wait_recv()
            if way == j:
                onward = copy(piece, piece, ids + 4 + way, where(turn if way == 0 else -turn))
                onward.start()
                started.append((None, onward))
            mates.append(mated(buf, place, j, ids + 6 + way * 2 + j, part))
        for one in mates:
            one.wait_recv()

    def ring_end(buf, ids, at, part):
        across = places(at)[2]
        mates = []
        for way in (0, 1):
            piece = buf.at[across, *part(way)]
            copy(piece, piece, ids + 4 + way, mate).wait_recv()
            mates.append(mated(buf, across, way, ids + 10 + way, part))
        return mates

    def done(mates):
        for one in mates:
            one.wait_recv()

    def whole(v):
        return jnp.concatenate([v[:128], jnp.concatenate([v[:128, 128:].T, v[128:, 128:]], 1)], 0)

    rows_256 = lax.broadcasted_iota(jnp.int32, (256, 256), 0)
    eye = (rows_256 == lax.broadcasted_iota(jnp.int32, (256, 256), 1)).astype(F32)

    def near_products(buf):
        rb[0] = eye
        rb[1] = buf[0]
        low = mm(split(buf[1]), split(buf[0]))
        rb[2] = low
        rb[3] = mm(split(buf[2]), split(low))

    def total_constant(buf, ring_mates, at):
        behind, ahead, across = places(at)
        total = jnp.zeros((256, 256), F32)
        for place in (at, behind, ahead):
            total = sandwich(rb[place], whole(buf[place]), total)
        done(ring_mates)
        return sandwich(rb[across], whole(buf[across]), total)

    def exclusive(links, consts, at, l_out, a_out):
        @pl.when(at == 3)
        def _():
            l_out[...] = eye
            a_out[...] = jnp.zeros((256, 256), F32)

        @pl.when(at < 3)
        def _():
            l_out[...] = links[3]
            a_out[...] = whole(consts[3])

        for i in (2, 1):

            @pl.when(at < i)
            def _():
                a_out[...] = sandwich(links[i], a_out[...], whole(consts[i]))
                l_out[...] = mm(split(l_out[...]), split(links[i]))

    cl_copy.wait_recv()
    yl[y] = mm(split(cl[1]), split(cl[0]))
    ring_send(yl, ID_YL, y, y_at, link_part)
    ca_copy.wait_recv()
    ya[y] = sandwich(cl[0], ca[1], ca[0])
    ring_send(ya, ID_YA, y, y_at, constant_part)

    ring_pass(yl, ID_YL, y, y_at, link_part)
    done(ring_end(yl, ID_YL, y, link_part))
    high = mm(split(yl[3]), split(yl[2]))
    low = mm(split(yl[1]), split(yl[0]))
    xl[x] = mm(split(high), split(low))
    ring_send(xl, ID_XL, x, x_at, link_part)
    near_products(yl)
    for p in (1, 0):
        z_take(fg, ID_ZF, p, 0)
        z_send(fg, ID_ZF, p, 1)
    ring_pass(ya, ID_YA, y, y_at, constant_part)
    xa[x] = total_constant(ya, ring_end(ya, ID_YA, y, constant_part), y)
    ring_send(xa, ID_XA, x, x_at, constant_part)

    ring_pass(xl, ID_XL, x, x_at, link_part)

    exclusive(yl, ya, y, el.at[1], ea.at[1])

    @pl.when(c == 0)
    def _():
        ea[1] = sandwich(cl[1], ea[1], ca[1])
        el[1] = mm(split(el[1]), split(cl[1]))

    ea[0] = sandwich(lp[1], ea[1], base[1])
    el[0] = mm(split(el[1]), split(lp[1]))

    done(ring_end(xl, ID_XL, x, link_part))
    for p in (1, 0):
        z_take(fg, ID_ZF, p, 1)
        z_send(fg, ID_ZF, p, 2)
    near_products(xl)
    ring_pass(xa, ID_XA, x, x_at, constant_part)

    hop = z_at(jnp.where(r == 0, -1, 1))

    def zh(j, kind):
        piece = ph.at[*constant_part(j)]
        if kind == 0:
            return copy(th.at[*constant_part(j)], piece, ID_ZH + j, hop)
        if kind == 1:
            return copy(piece, piece, ID_ZH + 2 + j, inward)
        return copy(piece, piece, ID_ZH + 4 + j, mate)

    sends_half = both(later, edge)
    xa_mates = ring_end(xa, ID_XA, x, constant_part)

    @pl.when(sends_half)
    def _():
        th[...] = total_constant(xa, xa_mates, x)
        for j in (0, 1):
            zh(j, 0).start()

    @pl.when(jnp.logical_not(sends_half))
    def _():
        done(xa_mates)

    for p in (1, 0):
        z_take(fg, ID_ZF, p, 2)
    exclusive(xl, xa, x, el.at[2], ea.at[2])
    for p in (1, 0):
        l_in = split(el[p])
        constant = sandwich(el[p], ea[2], ea[p])
        full = split(fg[p])
        mine = fg[p, :, pl.ds(pl.multiple_of(r * 128, 128), 128)]
        middle = mm(split(constant), split(mine))
        pb[...] = constant
        left = jnp.concatenate([middle.T, pb[pl.ds(r * 64, 64), :]], 0)
        out = mm(split(left), full)
        cov[p] += out[:128]
        off[p] = out[128:]

        @pl.when(h == 0)
        def _():
            link = mm(split(el[2]), l_in)
            pb[...] = link.T
            gg[p] = mm(split(link), full)
            kk[p * 192 : p * 192 + 128, :] = gg[p, :, pl.ds(pl.multiple_of(r * 128, 128), 128)].T
            kk[p * 192 + 128 : p * 192 + 192, :] = pb[pl.ds(r * 64, 64), :]

    @pl.when(both(h == 0, edge))
    def _():
        for j in (0, 1):
            zh(j, 0).wait_recv()
            zh(j, 1).start()
            zh(j, 2).start()

    @pl.when(both(h == 0, jnp.logical_not(edge)))
    def _():
        for j in (0, 1):
            zh(j, 1).wait_recv()
            zh(j, 2).start()

    @pl.when(h == 0)
    def _():
        for j in (0, 1):
            zh(j, 2).wait_recv()
        left = split(mm(split(kk[...]), split(whole(ph[...]))))
        for p in (0, 1):
            at = slice(p * 192, p * 192 + 192)
            out = mm((left[0][at], left[1][at]), split(gg[p]))
            cov[p] += out[:128]
            off[p] += out[128:]

    for p in (0, 1):
        off[p] = off[p] * (-mask[p, r].astype(F32))

    for sends, one in started:
        if sends is None:
            one.wait_send()
        else:

            @pl.when(sends)
            def _():
                one().wait_send()

    @pl.when(sends_half)
    def _():
        for j in (0, 1):
            zh(j, 0).wait_send()

    @pl.when(jnp.logical_and(h == 0, edge))
    def _():
        for j in (0, 1):
            zh(j, 1).wait_send()

    @pl.when(h == 0)
    def _():
        for j in (0, 1):
            zh(j, 2).wait_send()


def body(fill_blocks, fill_mask, inv_diag, factor_off):
    vmem = pl.BlockSpec(memory_space=pltpu.VMEM)

    def sq(n):
        return pltpu.VMEM((n, 256, 256), F32)

    return pl.pallas_call(
        kernel,
        name="chain",
        out_shape=(
            jax.ShapeDtypeStruct((2, 128, 512), F32),
            jax.ShapeDtypeStruct((2, 64, 512), F32),
        ),
        in_specs=[pl.BlockSpec(memory_space=pl.ANY)] * 4,
        out_specs=(vmem, vmem),
        scratch_shapes=[
            pltpu.SMEM((2, 4), jnp.int32),
            pltpu.SMEM((2, 4), jnp.int32),
            pltpu.VMEM((2, 512, 512), F32),
            pltpu.VMEM((2, 64, 512), F32),
            pltpu.SemaphoreType.DMA((5,)),
            pltpu.VMEM((8, 256), jnp.int32),
            pltpu.VMEM((8, 256), jnp.int32),
            pltpu.VMEM((2, 512, 512), BF16),
            pltpu.VMEM((2, 512, 512), BF16),
            sq(2),
            pltpu.VMEM((2, 256, 512), F32),
            sq(2),
            sq(2),
            sq(2),
            sq(4),
            sq(4),
            sq(4),
            sq(4),
            sq(3),
            sq(3),
            pltpu.VMEM((256, 256), F32),
            pltpu.VMEM((256, 256), F32),
            pltpu.VMEM((256, 256), F32),
            sq(4),
            pltpu.VMEM((2, 256, 512), F32),
            pltpu.VMEM((384, 256), F32),
            pltpu.SemaphoreType.DMA((N_IDS,)),
            pltpu.SemaphoreType.DMA((N_IDS,)),
        ],
        compiler_params=pltpu.CompilerParams(
            collective_id=0, has_side_effects=True
        ),
    )(fill_blocks, fill_mask, inv_diag, factor_off)


def solution(mesh):
    torus = Mesh(mesh.devices.reshape(2, 4, 4, 2, mesh.shape["row"]), (*SEG, "row"))
    placed = (P(SEG, None), P(SEG, None), P(SEG, None, None), P(SEG, "row", None))
    return jax.shard_map(
        body,
        mesh=torus,
        in_specs=placed,
        out_specs=(P(SEG, "row", None), P(SEG, "row", None)),
        check_vma=False,
    )
```

time: 83.4 us -> 75.3 us (0.903)
  Pallas kernels: 77.2 us -> 70.9 us
  local copies, waits for them, and re-layouts: 5.39 us -> 3.54 us
    pallas_call x1, Pallas kernels: 77.2 us -> 70.9 us  [body(): pl.pallas_call(kernel, name='chain', out_shape=(jax.ShapeDtypeStruct((2,...]
    unnamed x10 -> x2, local copies, waits for them, and re-layouts: 5.39 us -> 3.54 us
where the time goes in v2:
time: 75.3 us; the launch traced here: 75.1 us
  Pallas kernels  70.9 us (94%)
  local copies, waits for them, and re-layouts  3.54 us (5%)
    pallas_call x1, Pallas kernels, body(): pl.pallas_call(kernel, name='chain', out_shape=(jax.ShapeDtypeStruct((2,...  70.9 us
    unnamed x2, local copies, waits for them, and re-layouts  3.54 us

profile of v2, /device:TPU:33, one launch (start us, length us, event | category | flops | bytes accessed | tf_op | source)
XLA Modules:
  0.0 75.1 jit_solution(9784232455900917516)
XLA Ops:
  0.6 70.9 %chain.1 = (f32[2,128,512]{2,1,0:T(8,128)}, f32[2,64,512]{2,1,0:T(8,128)}) custom-call(s32[2,4]{1,0:T(2,128)} %blocks_hbm.1, s32[2,4]{1,0:T(2,128)} %mask_hbm.1, f32[2,512,512]{2,1,0:T(8,128)} %inv_hbm.1, f32[2,64,512]{2,1,0:T(8,128)} %fac_hbm.1), custom_call_target="tpu_custom_call" | custom-call | tf_op jit(solution)/shard_map/chain/pallas_call | solution.py:504
  71.6 1.9 %copy.8 = f32[2,128,512]{2,1,0:T(8,128)} copy(f32[2,128,512]{2,1,0:T(8,128)} %get-tuple-element.4) | data formatting | bytes 1048576
  73.4 1.7 %copy.9 = f32[2,64,512]{2,1,0:T(8,128)} copy(f32[2,64,512]{2,1,0:T(8,128)} %get-tuple-element.5) | data formatting | bytes 524288

commit v3 on v2

--- a/solution.py
+++ b/solution.py
@@ -219,8 +219,14 @@
             def _():
                 into().wait_recv()
 
+    def z_next(buf, ids, p, k):
+        z_take(buf, ids, p, k)
+        if k < 2:
+            z_send(buf, ids, p, k + 1)
+
     z_send(lp, ID_ZL, 1, 0)
     local_base(1, choose_1)
+    z_next(lp, ID_ZL, 1, 0)
 
     @pl.when(jnp.logical_or(plain_in, far_in))
     def _():
@@ -240,15 +246,14 @@
     local_link(0, choose_0)
     z_send(lp, ID_ZL, 0, 0)
     local_base(0, choose_0)
-    for k in range(3):
-        for p in (1, 0):
-            z_take(lp, ID_ZL, p, k)
-            if k < 2:
-                z_send(lp, ID_ZL, p, k + 1)
-        if k == 0:
-            for p in (0, 1):
-                mine = inv[p, :, pl.ds(pl.multiple_of(r * 128, 128), 128)]
-                cov[p] = mm(split(mine.T), (inv_h[p], inv_l[p]))
+    z_next(lp, ID_ZL, 1, 1)
+    z_next(lp, ID_ZL, 0, 0)
+    for p in (0, 1):
+        mine = inv[p, :, pl.ds(pl.multiple_of(r * 128, 128), 128)]
+        cov[p] = mm(split(mine.T), (inv_h[p], inv_l[p]))
+    z_next(lp, ID_ZL, 0, 1)
+    z_next(lp, ID_ZL, 1, 2)
+    z_next(lp, ID_ZL, 0, 2)
     for p in (1, 0):
         z_send(fg, ID_ZF, p, 0)
 
@@ -290,8 +295,8 @@
         started.append((None, one))
         return one
 
-    def ring_pass(buf, ids, at, where, part):
-        behind, ahead, across = places(at)
+    def direct(buf, ids, at, where, part):
+        behind, ahead, _ = places(at)
         mates = []
         for way, j in ((0, 0), (1, 1), (0, 1), (1, 0)):
             place = behind if way == 0 else ahead
@@ -302,10 +307,9 @@
                 onward.start()
                 started.append((None, onward))
             mates.append(mated(buf, place, j, ids + 6 + way * 2 + j, part))
-        for one in mates:
-            one.wait_recv()
-
-    def ring_end(buf, ids, at, part):
+        return mates
+
+    def opposite(buf, ids, at, part):
         across = places(at)[2]
         mates = []
         for way in (0, 1):
@@ -331,31 +335,38 @@
         rb[2] = low
         rb[3] = mm(split(buf[2]), split(low))
 
-    def total_constant(buf, ring_mates, at):
-        behind, ahead, across = places(at)
-        total = jnp.zeros((256, 256), F32)
-        for place in (at, behind, ahead):
-            total = sandwich(rb[place], whole(buf[place]), total)
-        done(ring_mates)
-        return sandwich(rb[across], whole(buf[across]), total)
-
-    def exclusive(links, consts, at, l_out, a_out):
+    def term(buf, place, added):
+        return sandwich(rb[place], whole(buf[place]), added)
+
+    def exclusive_links(links, at, out):
         @pl.when(at == 3)
         def _():
-            l_out[...] = eye
-            a_out[...] = jnp.zeros((256, 256), F32)
+            out[...] = eye
 
         @pl.when(at < 3)
         def _():
-            l_out[...] = links[3]
-            a_out[...] = whole(consts[3])
+            out[...] = links[3]
 
         for i in (2, 1):
 
             @pl.when(at < i)
             def _():
-                a_out[...] = sandwich(links[i], a_out[...], whole(consts[i]))
-                l_out[...] = mm(split(l_out[...]), split(links[i]))
+                out[...] = mm(split(out[...]), split(links[i]))
+
+    def exclusive_constants(links, consts, at, out):
+        @pl.when(at == 3)
+        def _():
+            out[...] = jnp.zeros((256, 256), F32)
+
+        @pl.when(at < 3)
+        def _():
+            out[...] = whole(consts[3])
+
+        for i in (2, 1):
+
+            @pl.when(at < i)
+            def _():
+                out[...] = sandwich(links[i], out[...], whole(consts[i]))
 
     cl_copy.wait_recv()
     yl[y] = mm(split(cl[1]), split(cl[0]))
@@ -364,23 +375,30 @@
     ya[y] = sandwich(cl[0], ca[1], ca[0])
     ring_send(ya, ID_YA, y, y_at, constant_part)
 
-    ring_pass(yl, ID_YL, y, y_at, link_part)
-    done(ring_end(yl, ID_YL, y, link_part))
+    yl_mates = direct(yl, ID_YL, y, y_at, link_part)
+    z_next(fg, ID_ZF, 1, 0)
+    z_next(fg, ID_ZF, 0, 0)
+    ya_mates = direct(ya, ID_YA, y, y_at, constant_part)
+    done(yl_mates + opposite(yl, ID_YL, y, link_part))
     high = mm(split(yl[3]), split(yl[2]))
     low = mm(split(yl[1]), split(yl[0]))
     xl[x] = mm(split(high), split(low))
     ring_send(xl, ID_XL, x, x_at, link_part)
+    z_next(fg, ID_ZF, 1, 1)
     near_products(yl)
-    for p in (1, 0):
-        z_take(fg, ID_ZF, p, 0)
-        z_send(fg, ID_ZF, p, 1)
-    ring_pass(ya, ID_YA, y, y_at, constant_part)
-    xa[x] = total_constant(ya, ring_end(ya, ID_YA, y, constant_part), y)
+    done(ya_mates)
+    behind, ahead, across = places(y)
+    total = term(ya, ahead, term(ya, y, jnp.zeros((256, 256), F32)))
+    ya_mates = opposite(ya, ID_YA, y, constant_part)
+    total = term(ya, behind, total)
+    done(ya_mates)
+    xa[x] = term(ya, across, total)
     ring_send(xa, ID_XA, x, x_at, constant_part)
 
-    ring_pass(xl, ID_XL, x, x_at, link_part)
-
-    exclusive(yl, ya, y, el.at[1], ea.at[1])
+    z_next(fg, ID_ZF, 0, 1)
+    exclusive_links(yl, y, el.at[1])
+    exclusive_constants(yl, ya, y, ea.at[1])
+    xl_mates = direct(xl, ID_XL, x, x_at, link_part)
 
     @pl.when(c == 0)
     def _():
@@ -390,12 +408,32 @@
     ea[0] = sandwich(lp[1], ea[1], base[1])
     el[0] = mm(split(el[1]), split(lp[1]))
 
-    done(ring_end(xl, ID_XL, x, link_part))
-    for p in (1, 0):
-        z_take(fg, ID_ZF, p, 1)
-        z_send(fg, ID_ZF, p, 2)
-    near_products(xl)
-    ring_pass(xa, ID_XA, x, x_at, constant_part)
+    xa_mates = direct(xa, ID_XA, x, x_at, constant_part)
+    done(xl_mates + opposite(xl, ID_XL, x, link_part))
+    sends_half = both(later, edge)
+    behind, ahead, across = places(x)
+    z_next(fg, ID_ZF, 1, 2)
+    z_next(fg, ID_ZF, 0, 2)
+    done(xa_mates)
+
+    @pl.when(sends_half)
+    def _():
+        near_products(xl)
+        zero = jnp.zeros((256, 256), F32)
+        th[...] = term(xa, behind, term(xa, ahead, term(xa, x, zero)))
+
+    @pl.when(h == 0)
+    def _():
+        exclusive_links(xl, x, el.at[2])
+        entry = split(el[2])
+        for p in (1, 0):
+            link = mm(entry, split(el[p]))
+            pb[...] = link.T
+            gg[p] = mm(split(link), split(fg[p]))
+            kk[p * 192 : p * 192 + 128, :] = gg[p, :, pl.ds(pl.multiple_of(r * 128, 128), 128)].T
+            kk[p * 192 + 128 : p * 192 + 192, :] = pb[pl.ds(r * 64, 64), :]
+
+    done(opposite(xa, ID_XA, x, constant_part))
 
     hop = z_at(jnp.where(r == 0, -1, 1))
 
@@ -407,41 +445,25 @@
             return copy(piece, piece, ID_ZH + 2 + j, inward)
         return copy(piece, piece, ID_ZH + 4 + j, mate)
 
-    sends_half = both(later, edge)
-    xa_mates = ring_end(xa, ID_XA, x, constant_part)
-
     @pl.when(sends_half)
     def _():
-        th[...] = total_constant(xa, xa_mates, x)
+        th[...] = term(xa, across, th[...])
         for j in (0, 1):
             zh(j, 0).start()
 
-    @pl.when(jnp.logical_not(sends_half))
-    def _():
-        done(xa_mates)
-
-    for p in (1, 0):
-        z_take(fg, ID_ZF, p, 2)
-    exclusive(xl, xa, x, el.at[2], ea.at[2])
-    for p in (1, 0):
-        l_in = split(el[p])
+    exclusive_constants(xl, xa, x, ea.at[2])
+
+    def outputs(p):
         constant = sandwich(el[p], ea[2], ea[p])
-        full = split(fg[p])
         mine = fg[p, :, pl.ds(pl.multiple_of(r * 128, 128), 128)]
         middle = mm(split(constant), split(mine))
         pb[...] = constant
         left = jnp.concatenate([middle.T, pb[pl.ds(r * 64, 64), :]], 0)
-        out = mm(split(left), full)
+        out = mm(split(left), split(fg[p]))
         cov[p] += out[:128]
         off[p] = out[128:]
 
-        @pl.when(h == 0)
-        def _():
-            link = mm(split(el[2]), l_in)
-            pb[...] = link.T
-            gg[p] = mm(split(link), full)
-            kk[p * 192 : p * 192 + 128, :] = gg[p, :, pl.ds(pl.multiple_of(r * 128, 128), 128)].T
-            kk[p * 192 + 128 : p * 192 + 192, :] = pb[pl.ds(r * 64, 64), :]
+    outputs(1)
 
     @pl.when(both(h == 0, edge))
     def _():
@@ -449,6 +471,8 @@
             zh(j, 0).wait_recv()
             zh(j, 1).start()
             zh(j, 2).start()
+
+    outputs(0)
 
     @pl.when(both(h == 0, jnp.logical_not(edge)))
     def _():

time: 75.3 us -> 67.3 us (0.89)
  Pallas kernels: 70.9 us -> 62.6 us
    pallas_call x1, Pallas kernels: 70.9 us -> 62.6 us  [body(): pl.pallas_call(kernel, name='chain', out_shape=(jax.ShapeDtypeStruct((2,...]
where the time goes in v3:
time: 67.3 us; the launch traced here: 66.7 us
  Pallas kernels  62.6 us (93%)
  local copies, waits for them, and re-layouts  3.54 us (5%)
    pallas_call x1, Pallas kernels, body(): pl.pallas_call(kernel, name='chain', out_shape=(jax.ShapeDtypeStruct((2,...  62.6 us
    unnamed x2, local copies, waits for them, and re-layouts  3.54 us

profile of v3, /device:TPU:33, one launch (start us, length us, event | category | flops | bytes accessed | tf_op | source)
XLA Modules:
  0.0 66.7 jit_solution(11198351344170530501)
XLA Ops:
  0.6 62.6 %chain.1 = (f32[2,128,512]{2,1,0:T(8,128)}, f32[2,64,512]{2,1,0:T(8,128)}) custom-call(s32[2,4]{1,0:T(2,128)} %blocks_hbm.1, s32[2,4]{1,0:T(2,128)} %mask_hbm.1, f32[2,512,512]{2,1,0:T(8,128)} %inv_hbm.1, f32[2,64,512]{2,1,0:T(8,128)} %fac_hbm.1), custom_call_target="tpu_custom_call" | custom-call | tf_op jit(solution)/shard_map/chain/pallas_call | solution.py:528
  63.2 1.9 %copy.8 = f32[2,128,512]{2,1,0:T(8,128)} copy(f32[2,128,512]{2,1,0:T(8,128)} %get-tuple-element.4) | data formatting | bytes 1048576
  65.1 1.7 %copy.9 = f32[2,64,512]{2,1,0:T(8,128)} copy(f32[2,64,512]{2,1,0:T(8,128)} %get-tuple-element.5) | data formatting | bytes 524288

commit v4 on v3

--- a/solution.py
+++ b/solution.py
@@ -21,6 +21,7 @@
 ID_YA = 39
 ID_XL = 51
 ID_XA = 63
+ID_ZL_LATE = 84
 ID_RELAY = 99
 ID_ZH = 75
 
@@ -47,12 +48,14 @@
 def kernel(
     blocks_hbm, mask_hbm, inv_hbm, fac_hbm, cov, off,
     blocks, mask, inv, fac, local, idx_out, idx_in, inv_h, inv_l, lp, fg, base, cl, ca, yl, ya, xl, xa,
-    el, ea, ph, th, pb, rb, gg, kk, ss, rs,
+    el, ea, ph, th, pb, rb, sm, gg, kk, ss, rs,
 ):
     h, x, y, c = (lax.axis_index(a) for a in SEG)
     r = lax.axis_index("row")
     z = 4 * h + r
     seg = ((h * 4 + x) * 4 + y) * 2 + c
+
+    both = jnp.logical_and
 
     def z_at(d):
         zz = lax.rem(z + d + 8, 8)
@@ -83,7 +86,6 @@
     for who in (mate, z_at(1), z_at(-1), y_at(1), y_at(-1), x_at(1), x_at(-1)):
         greet(who)
 
-    both = jnp.logical_and
     later = h == 1
     edge = jnp.logical_or(r == 0, r == 3)
     tail = both(both(x == 3, y == 3), c == 1)
@@ -97,7 +99,7 @@
         "seg_3": 1 - c, "row": 3 - r,
     }
     for cond, who in (
-        (plain_out, seg_at(1)), (plain_in, seg_at(-1)), (far_out, across_half), (far_in, across_half),
+        (plain_in, seg_at(-1)), (far_in, across_half),
     ):
 
         @pl.when(cond)
@@ -105,7 +107,7 @@
             greet(who)
 
     greetings = 7
-    for cond in (plain_out, plain_in, far_out, far_in):
+    for cond in (plain_out, far_out):
         greetings = greetings + jnp.where(cond, 1, 0)
 
     loads = [
@@ -187,7 +189,7 @@
     inward = z_at(jnp.where(r == 0, 1, -1))
     relay = lambda: copy(idx_in, idx_in, ID_RELAY, inward)
 
-    def z_parts(buf, ids, p, k, up):
+    def z_parts(buf, ids, p, k, up, lo, n):
         block = (r - k) if up else (r + k)
         block_in = (r - 1 - k) if up else (r + 1 + k)
         sends = jnp.logical_and(r < 3, r - k >= 0) if up else jnp.logical_and(r > 0, r + k <= 3)
@@ -196,14 +198,16 @@
         who = z_at(1 if up else -1)
 
         def made(b):
-            part = buf.at[p, pl.ds(b * 64, 64), :]
+            part = buf.at[p, pl.ds(b * 64 + lo, n), :]
             return copy(part, part, number, who)
 
         return sends, takes, lambda: made(block), lambda: made(block_in)
 
-    def z_send(buf, ids, p, k):
+    def z_send(buf, ids, p, k, lo=0, n=64, cond=None):
         for up in (True, False):
-            sends, _, out, _ = z_parts(buf, ids, p, k, up)
+            sends, _, out, _ = z_parts(buf, ids, p, k, up, lo, n)
+            if cond is not None:
+                sends = both(sends, cond)
 
             @pl.when(sends)
             def _():
@@ -211,22 +215,28 @@
 
             started.append((sends, out))
 
-    def z_take(buf, ids, p, k):
+    def z_take(buf, ids, p, k, lo=0, n=64, cond=None):
         for up in (True, False):
-            _, takes, _, into = z_parts(buf, ids, p, k, up)
+            _, takes, _, into = z_parts(buf, ids, p, k, up, lo, n)
+            if cond is not None:
+                takes = both(takes, cond)
 
             @pl.when(takes)
             def _():
                 into().wait_recv()
 
-    def z_next(buf, ids, p, k):
-        z_take(buf, ids, p, k)
+    def z_next(buf, ids, p, k, lo=0, n=64, cond=None):
+        z_take(buf, ids, p, k, lo, n, cond)
         if k < 2:
-            z_send(buf, ids, p, k + 1)
+            z_send(buf, ids, p, k + 1, lo, n, cond)
+
+    halves = ((ID_ZL, 0), (ID_ZL_LATE, 32))
+    waits_long = both(head, later)
 
     z_send(lp, ID_ZL, 1, 0)
     local_base(1, choose_1)
     z_next(lp, ID_ZL, 1, 0)
+    z_next(lp, ID_ZL, 1, 1, cond=waits_long)
 
     @pl.when(jnp.logical_or(plain_in, far_in))
     def _():
@@ -244,16 +254,20 @@
 
     choose_0 = chooser(idx_in[...])
     local_link(0, choose_0)
-    z_send(lp, ID_ZL, 0, 0)
+    for ids, lo in halves:
+        z_send(lp, ids, 0, 0, lo, 32)
     local_base(0, choose_0)
-    z_next(lp, ID_ZL, 1, 1)
-    z_next(lp, ID_ZL, 0, 0)
+    z_next(lp, ID_ZL, 1, 1, cond=jnp.logical_not(waits_long))
+    for ids, lo in halves:
+        z_next(lp, ids, 0, 0, lo, 32)
     for p in (0, 1):
         mine = inv[p, :, pl.ds(pl.multiple_of(r * 128, 128), 128)]
         cov[p] = mm(split(mine.T), (inv_h[p], inv_l[p]))
-    z_next(lp, ID_ZL, 0, 1)
+    for ids, lo in halves:
+        z_next(lp, ids, 0, 1, lo, 32)
     z_next(lp, ID_ZL, 1, 2)
-    z_next(lp, ID_ZL, 0, 2)
+    for ids, lo in halves:
+        z_next(lp, ids, 0, 2, lo, 32)
     for p in (1, 0):
         z_send(fg, ID_ZF, p, 0)
 
@@ -379,20 +393,53 @@
     z_next(fg, ID_ZF, 1, 0)
     z_next(fg, ID_ZF, 0, 0)
     ya_mates = direct(ya, ID_YA, y, y_at, constant_part)
-    done(yl_mates + opposite(yl, ID_YL, y, link_part))
+    done(yl_mates)
+    done(ya_mates)
+
+    @pl.when(y == 0)
+    def _():
+        rb[2] = mm(split(yl[1]), split(yl[0]))
+        sm[...] = sandwich(yl[0], whole(ya[1]), whole(ya[0]))
+
+    @pl.when(y == 1)
+    def _():
+        low = mm(split(yl[1]), split(yl[0]))
+        near = sandwich(yl[0], whole(ya[1]), whole(ya[0]))
+        rb[3] = mm(split(yl[2]), split(low))
+        sm[...] = sandwich(low, whole(ya[2]), near)
+
+    @pl.when(y == 2)
+    def _():
+        rb[0] = eye
+        sm[...] = sandwich(yl[1], sandwich(yl[2], whole(ya[3]), whole(ya[2])), whole(ya[1]))
+
+    @pl.when(y == 3)
+    def _():
+        rb[1] = yl[0]
+        sm[...] = sandwich(yl[2], whole(ya[3]), whole(ya[2]))
+
+    done(opposite(yl, ID_YL, y, link_part))
     high = mm(split(yl[3]), split(yl[2]))
     low = mm(split(yl[1]), split(yl[0]))
     xl[x] = mm(split(high), split(low))
     ring_send(xl, ID_XL, x, x_at, link_part)
     z_next(fg, ID_ZF, 1, 1)
-    near_products(yl)
-    done(ya_mates)
-    behind, ahead, across = places(y)
-    total = term(ya, ahead, term(ya, y, jnp.zeros((256, 256), F32)))
-    ya_mates = opposite(ya, ID_YA, y, constant_part)
-    total = term(ya, behind, total)
-    done(ya_mates)
-    xa[x] = term(ya, across, total)
+
+    @pl.when(y == 0)
+    def _():
+        sm[...] = sandwich(mm(split(yl[2]), split(rb[2])), whole(ya[3]), sm[...])
+
+    @pl.when(y == 2)
+    def _():
+        sm[...] = sandwich(yl[0], sm[...], jnp.zeros((256, 256), F32))
+
+    @pl.when(y == 3)
+    def _():
+        sm[...] = sandwich(mm(split(yl[1]), split(yl[0])), sm[...], whole(ya[0]))
+
+    across = places(y)[2]
+    done(opposite(ya, ID_YA, y, constant_part))
+    xa[x] = term(ya, across, sm[...])
     ring_send(xa, ID_XA, x, x_at, constant_part)
 
     z_next(fg, ID_ZF, 0, 1)
@@ -438,17 +485,19 @@
     hop = z_at(jnp.where(r == 0, -1, 1))
 
     def zh(j, kind):
-        piece = ph.at[*constant_part(j)]
+        if j < 2:
+            part = pl.ds(c * 128 + j * 64, 64), pl.ds(pl.multiple_of(c * 128, 128), 128)
+        else:
+            part = pl.ds(c * 64, 64), pl.ds(128, 128)
+        piece = ph.at[*part]
         if kind == 0:
-            return copy(th.at[*constant_part(j)], piece, ID_ZH + j, hop)
-        if kind == 1:
-            return copy(piece, piece, ID_ZH + 2 + j, inward)
-        return copy(piece, piece, ID_ZH + 4 + j, mate)
+            return copy(th.at[*part], piece, ID_ZH + j, hop)
+        return copy(piece, piece, ID_ZH + 3 * kind + j, inward if kind == 1 else mate)
 
     @pl.when(sends_half)
     def _():
         th[...] = term(xa, across, th[...])
-        for j in (0, 1):
+        for j in (0, 1, 2):
             zh(j, 0).start()
 
     exclusive_constants(xl, xa, x, ea.at[2])
@@ -467,7 +516,7 @@
 
     @pl.when(both(h == 0, edge))
     def _():
-        for j in (0, 1):
+        for j in (0, 1, 2):
             zh(j, 0).wait_recv()
             zh(j, 1).start()
             zh(j, 2).start()
@@ -476,13 +525,13 @@
 
     @pl.when(both(h == 0, jnp.logical_not(edge)))
     def _():
-        for j in (0, 1):
+        for j in (0, 1, 2):
             zh(j, 1).wait_recv()
             zh(j, 2).start()
 
     @pl.when(h == 0)
     def _():
-        for j in (0, 1):
+        for j in (0, 1, 2):
             zh(j, 2).wait_recv()
         left = split(mm(split(kk[...]), split(whole(ph[...]))))
         for p in (0, 1):
@@ -505,17 +554,17 @@
 
     @pl.when(sends_half)
     def _():
-        for j in (0, 1):
+        for j in (0, 1, 2):
             zh(j, 0).wait_send()
 
     @pl.when(jnp.logical_and(h == 0, edge))
     def _():
-        for j in (0, 1):
+        for j in (0, 1, 2):
             zh(j, 1).wait_send()
 
     @pl.when(h == 0)
     def _():
-        for j in (0, 1):
+        for j in (0, 1, 2):
             zh(j, 2).wait_send()
 
 
@@ -559,6 +608,7 @@
             pltpu.VMEM((256, 256), F32),
             pltpu.VMEM((256, 256), F32),
             sq(4),
+            pltpu.VMEM((256, 256), F32),
             pltpu.VMEM((2, 256, 512), F32),
             pltpu.VMEM((384, 256), F32),
             pltpu.SemaphoreType.DMA((N_IDS,)),

time: 67.3 us -> 67.5 us (level); the launches traced: 66.7 us -> 66.2 us
  no operation moved by 1% of the time
where the time goes in v4:
time: 67.5 us; the launch traced here: 66.2 us
  Pallas kernels  62 us (92%)
  local copies, waits for them, and re-layouts  3.54 us (5%)
    pallas_call x1, Pallas kernels, body(): pl.pallas_call(kernel, name='chain', out_shape=(jax.ShapeDtypeStruct((2,...  62 us
    unnamed x2, local copies, waits for them, and re-layouts  3.54 us

profile of v4, /device:TPU:33, one launch (start us, length us, event | category | flops | bytes accessed | tf_op | source)
XLA Modules:
  0.0 66.2 jit_solution(12922188208007721784)
XLA Ops:
  0.6 62.0 %chain.1 = (f32[2,128,512]{2,1,0:T(8,128)}, f32[2,64,512]{2,1,0:T(8,128)}) custom-call(s32[2,4]{1,0:T(2,128)} %blocks_hbm.1, s32[2,4]{1,0:T(2,128)} %mask_hbm.1, f32[2,512,512]{2,1,0:T(8,128)} %inv_hbm.1, f32[2,64,512]{2,1,0:T(8,128)} %fac_hbm.1), custom_call_target="tpu_custom_call" | custom-call | tf_op jit(solution)/shard_map/chain/pallas_call | solution.py:577
  62.6 1.9 %copy.8 = f32[2,128,512]{2,1,0:T(8,128)} copy(f32[2,128,512]{2,1,0:T(8,128)} %get-tuple-element.4) | data formatting | bytes 1048576
  64.5 1.7 %copy.9 = f32[2,64,512]{2,1,0:T(8,128)} copy(f32[2,64,512]{2,1,0:T(8,128)} %get-tuple-element.5) | data formatting | bytes 524288

commit v5 on v4

--- a/solution.py
+++ b/solution.py
@@ -22,6 +22,7 @@
 ID_XL = 51
 ID_XA = 63
 ID_ZL_LATE = 84
+ID_ZF_LATE = 90
 ID_RELAY = 99
 ID_ZH = 75
 
@@ -114,7 +115,7 @@
         pltpu.make_async_copy(src, dst, local.at[i])
         for i, (src, dst) in enumerate((
             (blocks_hbm, blocks), (mask_hbm, mask), (fac_hbm, fac),
-            (inv_hbm.at[1], inv.at[1]), (inv_hbm.at[0], inv.at[0]),
+            (inv_hbm.at[c], inv.at[c]), (inv_hbm.at[1 - c], inv.at[1 - c]),
         ))
     ]
     for load in loads:
@@ -152,14 +153,11 @@
         live = mask[panel, r].astype(F32)
         return jnp.where(seg * 2 + panel < 127, live, 0.0)
 
-    frows = [None, None]
-    for p in (1, 0):
-        loads[4 - p].wait()
+    def factor_rows(p):
         ih, il = split(inv[p])
         inv_h[p] = ih
         inv_l[p] = il
-        frows[p] = mm(split(fac[p] * keep(p)), (ih, il))
-        fg[p, pl.ds(r * 64, 64), :] = frows[p]
+        fg[p, pl.ds(r * 64, 64), :] = mm(split(fac[p] * keep(p)), (ih, il))
 
     def local_link(p, choose):
         fh, fl = split(fg[p, pl.ds(r * 64, 64), :])
@@ -172,8 +170,13 @@
         cth, ctl = ch.T.astype(BF16), cl_.T.astype(BF16)
         base[p] = mm((cth, ctl), (chh, cll))
 
-    choose_1 = chooser(target_1)
-    local_link(1, choose_1)
+    is_a, is_b = c == 0, c == 1
+    loads[3].wait()
+    factor_rows(c)
+
+    @pl.when(is_b)
+    def _():
+        local_link(1, chooser(target_1))
 
     pl.semaphore_wait(barrier, greetings)
 
@@ -187,6 +190,11 @@
     begin(plain_out, lambda: copy(idx_out, idx_in, ID_IDX, seg_at(1)))
     begin(far_out, lambda: copy(idx_out, idx_in, ID_IDX, across_half))
     inward = z_at(jnp.where(r == 0, 1, -1))
+
+    @pl.when(both(head, h == 0))
+    def _():
+        idx_in[...] = target_1
+
     relay = lambda: copy(idx_in, idx_in, ID_RELAY, inward)
 
     def z_parts(buf, ids, p, k, up, lo, n):
@@ -230,46 +238,75 @@
         if k < 2:
             z_send(buf, ids, p, k + 1, lo, n, cond)
 
-    halves = ((ID_ZL, 0), (ID_ZL_LATE, 32))
     waits_long = both(head, later)
-
-    z_send(lp, ID_ZL, 1, 0)
-    local_base(1, choose_1)
-    z_next(lp, ID_ZL, 1, 0)
-    z_next(lp, ID_ZL, 1, 1, cond=waits_long)
-
-    @pl.when(jnp.logical_or(plain_in, far_in))
+    units = (
+        (fg, ID_ZF, 0, 0, 32, is_a), (fg, ID_ZF_LATE, 0, 32, 32, is_a),
+        (lp, ID_ZL, 1, 0, 64, None),
+        (lp, ID_ZL, 0, 0, 32, is_b), (lp, ID_ZL_LATE, 0, 32, 32, is_b),
+    )
+
+    def every(k):
+        for buf, ids, p, lo, n, cond in units:
+            z_next(buf, ids, p, k, lo, n, cond)
+
+    for buf, ids, p, lo, n, cond in units[:2]:
+        z_send(buf, ids, p, 0, lo, n, cond)
+    z_send(lp, ID_ZL, 1, 0, cond=is_b)
+    loads[4].wait()
+    factor_rows(1 - c)
+
+    @pl.when(is_a)
+    def _():
+        local_link(1, chooser(target_1))
+
+    z_send(lp, ID_ZL, 1, 0, cond=is_a)
+
+    @pl.when(is_b)
     def _():
         copy(idx_out, idx_in, ID_IDX, mate).wait_recv()
+        local_link(0, chooser(idx_in[...]))
+
+    for buf, ids, p, lo, n, cond in units[3:]:
+        z_send(buf, ids, p, 0, lo, n, cond)
+    local_base(1, chooser(target_1))
+    every(0)
+
+    @pl.when(both(is_a, plain_in))
+    def _():
+        copy(idx_out, idx_in, ID_IDX, mate).wait_recv()
+
+    @pl.when(jnp.logical_not(waits_long))
+    def _():
+        local_base(0, chooser(idx_in[...]))
+
+    every(1)
+
+    @pl.when(far_in)
+    def _():
+        copy(idx_out, idx_in, ID_IDX, mate).wait_recv()
 
     begin(far_in, relay)
-
-    @pl.when(relay_in)
-    def _():
-        relay().wait_recv()
-
-    @pl.when(both(head, h == 0))
-    def _():
-        idx_in[...] = target_1
-
-    choose_0 = chooser(idx_in[...])
-    local_link(0, choose_0)
-    for ids, lo in halves:
-        z_send(lp, ids, 0, 0, lo, 32)
-    local_base(0, choose_0)
-    z_next(lp, ID_ZL, 1, 1, cond=jnp.logical_not(waits_long))
-    for ids, lo in halves:
-        z_next(lp, ids, 0, 0, lo, 32)
     for p in (0, 1):
         mine = inv[p, :, pl.ds(pl.multiple_of(r * 128, 128), 128)]
         cov[p] = mm(split(mine.T), (inv_h[p], inv_l[p]))
-    for ids, lo in halves:
-        z_next(lp, ids, 0, 1, lo, 32)
-    z_next(lp, ID_ZL, 1, 2)
-    for ids, lo in halves:
-        z_next(lp, ids, 0, 2, lo, 32)
-    for p in (1, 0):
-        z_send(fg, ID_ZF, p, 0)
+    every(2)
+
+    @pl.when(relay_in)
+    def _():
+        relay().wait_recv()
+
+    @pl.when(waits_long)
+    def _():
+        local_base(0, chooser(idx_in[...]))
+
+    @pl.when(is_a)
+    def _():
+        fh, fl = split(fg[0])
+        choose = chooser(idx_in[...])
+        lp[0] = dot(fh, choose) + dot(fl, choose)
+
+    z_send(fg, ID_ZF, 1, 0)
+    z_send(fg, ID_ZF, 0, 0, cond=is_b)
 
     link_0 = split(lp[0])
     cl[c] = mm(split(lp[1]), link_0)
@@ -391,7 +428,7 @@
 
     yl_mates = direct(yl, ID_YL, y, y_at, link_part)
     z_next(fg, ID_ZF, 1, 0)
-    z_next(fg, ID_ZF, 0, 0)
+    z_next(fg, ID_ZF, 0, 0, cond=is_b)
     ya_mates = direct(ya, ID_YA, y, y_at, constant_part)
     done(yl_mates)
     done(ya_mates)
@@ -442,7 +479,7 @@
     xa[x] = term(ya, across, sm[...])
     ring_send(xa, ID_XA, x, x_at, constant_part)
 
-    z_next(fg, ID_ZF, 0, 1)
+    z_next(fg, ID_ZF, 0, 1, cond=is_b)
     exclusive_links(yl, y, el.at[1])
     exclusive_constants(yl, ya, y, ea.at[1])
     xl_mates = direct(xl, ID_XL, x, x_at, link_part)
@@ -460,7 +497,7 @@
     sends_half = both(later, edge)
     behind, ahead, across = places(x)
     z_next(fg, ID_ZF, 1, 2)
-    z_next(fg, ID_ZF, 0, 2)
+    z_next(fg, ID_ZF, 0, 2, cond=is_b)
     done(xa_mates)
 
     @pl.when(sends_half)

time: 67.5 us -> 66.4 us (0.984); the launches traced: 66.2 us -> 66.2 us
  no operation moved by 1% of the time
where the time goes in v5:
time: 66.4 us; the launch traced here: 66.2 us
  Pallas kernels  62 us (93%)
  local copies, waits for them, and re-layouts  3.54 us (5%)
    pallas_call x1, Pallas kernels, body(): pl.pallas_call(kernel, name='chain', out_shape=(jax.ShapeDtypeStruct((2,...  62 us
    unnamed x2, local copies, waits for them, and re-layouts  3.54 us

profile of v5, /device:TPU:33, one launch (start us, length us, event | category | flops | bytes accessed | tf_op | source)
XLA Modules:
  0.0 66.2 jit_solution(14670290500804322344)
XLA Ops:
  0.6 62.0 %chain.1 = (f32[2,128,512]{2,1,0:T(8,128)}, f32[2,64,512]{2,1,0:T(8,128)}) custom-call(s32[2,4]{1,0:T(2,128)} %blocks_hbm.1, s32[2,4]{1,0:T(2,128)} %mask_hbm.1, f32[2,512,512]{2,1,0:T(8,128)} %inv_hbm.1, f32[2,64,512]{2,1,0:T(8,128)} %fac_hbm.1), custom_call_target="tpu_custom_call" | custom-call | tf_op jit(solution)/shard_map/chain/pallas_call | solution.py:614
  62.7 1.9 %copy.8 = f32[2,128,512]{2,1,0:T(8,128)} copy(f32[2,128,512]{2,1,0:T(8,128)} %get-tuple-element.4) | data formatting | bytes 1048576
  64.6 1.7 %copy.9 = f32[2,64,512]{2,1,0:T(8,128)} copy(f32[2,64,512]{2,1,0:T(8,128)} %get-tuple-element.5) | data formatting | bytes 524288

commit v6 on v5

--- a/solution.py
+++ b/solution.py
@@ -480,24 +480,29 @@
     ring_send(xa, ID_XA, x, x_at, constant_part)
 
     z_next(fg, ID_ZF, 0, 1, cond=is_b)
-    exclusive_links(yl, y, el.at[1])
-    exclusive_constants(yl, ya, y, ea.at[1])
+
+    def group_map():
+        exclusive_links(yl, y, el.at[1])
+        exclusive_constants(yl, ya, y, ea.at[1])
+
+    def panel_maps():
+        @pl.when(c == 0)
+        def _():
+            ea[1] = sandwich(cl[1], ea[1], ca[1])
+            el[1] = mm(split(el[1]), split(cl[1]))
+
+        ea[0] = sandwich(lp[1], ea[1], base[1])
+        el[0] = mm(split(el[1]), split(lp[1]))
+
+    pl.when(h == 0)(group_map)
     xl_mates = direct(xl, ID_XL, x, x_at, link_part)
-
-    @pl.when(c == 0)
-    def _():
-        ea[1] = sandwich(cl[1], ea[1], ca[1])
-        el[1] = mm(split(el[1]), split(cl[1]))
-
-    ea[0] = sandwich(lp[1], ea[1], base[1])
-    el[0] = mm(split(el[1]), split(lp[1]))
-
+    pl.when(h == 0)(panel_maps)
     xa_mates = direct(xa, ID_XA, x, x_at, constant_part)
     done(xl_mates + opposite(xl, ID_XL, x, link_part))
     sends_half = both(later, edge)
     behind, ahead, across = places(x)
-    z_next(fg, ID_ZF, 1, 2)
-    z_next(fg, ID_ZF, 0, 2, cond=is_b)
+    z_next(fg, ID_ZF, 1, 2, cond=h == 0)
+    z_next(fg, ID_ZF, 0, 2, cond=both(is_b, h == 0))
     done(xa_mates)
 
     @pl.when(sends_half)
@@ -536,6 +541,14 @@
         th[...] = term(xa, across, th[...])
         for j in (0, 1, 2):
             zh(j, 0).start()
+
+    z_next(fg, ID_ZF, 1, 2, cond=later)
+    z_next(fg, ID_ZF, 0, 2, cond=both(is_b, later))
+
+    @pl.when(later)
+    def _():
+        group_map()
+        panel_maps()
 
     exclusive_constants(xl, xa, x, ea.at[2])
 

time: 66.4 us -> 66.4 us (level)
  no operation moved by 1% of the time
where the time goes in v6:
time: 66.4 us; the launch traced here: 66.2 us
  Pallas kernels  62 us (93%)
  local copies, waits for them, and re-layouts  3.54 us (5%)
    pallas_call x1, Pallas kernels, body(): pl.pallas_call(kernel, name='chain', out_shape=(jax.ShapeDtypeStruct((2,...  62 us
    unnamed x2, local copies, waits for them, and re-layouts  3.54 us

profile of v6, /device:TPU:33, one launch (start us, length us, event | category | flops | bytes accessed | tf_op | source)
XLA Modules:
  0.0 66.2 jit_solution(3150628776769310407)
XLA Ops:
  0.6 62.0 %chain.1 = (f32[2,128,512]{2,1,0:T(8,128)}, f32[2,64,512]{2,1,0:T(8,128)}) custom-call(s32[2,4]{1,0:T(2,128)} %blocks_hbm.1, s32[2,4]{1,0:T(2,128)} %mask_hbm.1, f32[2,512,512]{2,1,0:T(8,128)} %inv_hbm.1, f32[2,64,512]{2,1,0:T(8,128)} %fac_hbm.1), custom_call_target="tpu_custom_call" | custom-call | tf_op jit(solution)/shard_map/chain/pallas_call | solution.py:627
  62.7 1.9 %copy.8 = f32[2,128,512]{2,1,0:T(8,128)} copy(f32[2,128,512]{2,1,0:T(8,128)} %get-tuple-element.4) | data formatting | bytes 1048576
  64.6 1.7 %copy.9 = f32[2,64,512]{2,1,0:T(8,128)} copy(f32[2,64,512]{2,1,0:T(8,128)} %get-tuple-element.5) | data formatting | bytes 524288

commit v7 on v5

--- a/solution.py
+++ b/solution.py
@@ -78,6 +78,16 @@
         return {"seg_1": lax.rem(x + d + 4, 4)}
 
     mate = {"seg_3": 1 - c}
+
+    loads = [
+        pltpu.make_async_copy(src, dst, local.at[i])
+        for i, (src, dst) in enumerate((
+            (blocks_hbm, blocks), (mask_hbm, mask), (fac_hbm, fac),
+            (inv_hbm.at[c], inv.at[c]), (inv_hbm.at[1 - c], inv.at[1 - c]),
+        ))
+    ]
+    for load in loads:
+        load.start()
 
     barrier = pltpu.get_barrier_semaphore()
 
@@ -111,16 +121,6 @@
     for cond in (plain_out, far_out):
         greetings = greetings + jnp.where(cond, 1, 0)
 
-    loads = [
-        pltpu.make_async_copy(src, dst, local.at[i])
-        for i, (src, dst) in enumerate((
-            (blocks_hbm, blocks), (mask_hbm, mask), (fac_hbm, fac),
-            (inv_hbm.at[c], inv.at[c]), (inv_hbm.at[1 - c], inv.at[1 - c]),
-        ))
-    ]
-    for load in loads:
-        load.start()
-
     started = []
 
     def copy(src, dst, number, who):
@@ -614,11 +614,8 @@
     return pl.pallas_call(
         kernel,
         name="chain",
-        out_shape=(
-            jax.ShapeDtypeStruct((2, 128, 512), F32),
-            jax.ShapeDtypeStruct((2, 64, 512), F32),
-        ),
-        in_specs=[pl.BlockSpec(memory_space=pl.ANY)] * 4,
+        out_shape=(pltpu.VMEM((2, 128, 512), F32), pltpu.VMEM((2, 64, 512), F32)),
+        in_specs=[pl.BlockSpec(memory_space=pltpu.HBM)] * 4,
         out_specs=(vmem, vmem),
         scratch_shapes=[
             pltpu.SMEM((2, 4), jnp.int32),

time: 66.4 us -> 63.1 us (0.950)
  local copies, waits for them, and re-layouts: 3.54 us -> 1.5 us
  Pallas kernels: 62 us -> 60.9 us
    unnamed x2, local copies, waits for them, and re-layouts: 3.54 us -> 1.5 us
    pallas_call x1, Pallas kernels: 62 us -> 60.9 us  [body(): pl.pallas_call(kernel, name='chain', out_shape=(pltpu.VMEM((2, 128, 512),...]
where the time goes in v7:
time: 63.1 us; the launch traced here: 63 us
  Pallas kernels  60.9 us (97%)
  local copies, waits for them, and re-layouts  1.5 us (2%)
  between operations  0.64 us (1%)
    pallas_call x1, Pallas kernels, body(): pl.pallas_call(kernel, name='chain', out_shape=(pltpu.VMEM((2, 128, 512),...  60.9 us
    unnamed x2, local copies, waits for them, and re-layouts  1.5 us

profile of v7, /device:TPU:33, one launch (start us, length us, event | category | flops | bytes accessed | tf_op | source)
XLA Modules:
  0.0 63.0 jit_solution(10929167440753024890)
XLA Ops:
  0.6 60.9 %chain.1 = (f32[2,128,512]{2,1,0:T(8,128)S(1)}, f32[2,64,512]{2,1,0:T(8,128)S(1)}) custom-call(s32[2,4]{1,0:T(2,128)} %blocks_hbm.1, s32[2,4]{1,0:T(2,128)} %mask_hbm.1, f32[2,512,512]{2,1,0:T(8,128)} %inv_hbm.1, f32[2,64,512]{2,1,0:T(8,128)} %fac_hbm.1), custom_call_target="tpu_custom_call" | custom-call | tf_op jit(solution)/shard_map/chain/pallas_call | solution.py:614
  61.5 0.8 %copy.8 = f32[2,128,512]{2,1,0:T(8,128)} copy(f32[2,128,512]{2,1,0:T(8,128)S(1)} %get-tuple-element.2) | data formatting | bytes 1048576
  62.3 0.7 %copy.9 = f32[2,64,512]{2,1,0:T(8,128)} copy(f32[2,64,512]{2,1,0:T(8,128)S(1)} %get-tuple-element.3) | data formatting | bytes 524288

commit v8 on v7

--- a/solution.py
+++ b/solution.py
@@ -605,13 +605,24 @@
             zh(j, 2).wait_send()
 
 
+def put_out(cov, off, cov_out, off_out, sems):
+    copies = (
+        pltpu.make_async_copy(cov, cov_out, sems.at[0]),
+        pltpu.make_async_copy(off, off_out, sems.at[1]),
+    )
+    for one in copies:
+        one.start()
+    for one in copies:
+        one.wait()
+
+
 def body(fill_blocks, fill_mask, inv_diag, factor_off):
     vmem = pl.BlockSpec(memory_space=pltpu.VMEM)
 
     def sq(n):
         return pltpu.VMEM((n, 256, 256), F32)
 
-    return pl.pallas_call(
+    results = pl.pallas_call(
         kernel,
         name="chain",
         out_shape=(pltpu.VMEM((2, 128, 512), F32), pltpu.VMEM((2, 64, 512), F32)),
@@ -652,6 +663,19 @@
             collective_id=0, has_side_effects=True
         ),
     )(fill_blocks, fill_mask, inv_diag, factor_off)
+    hbm = pl.BlockSpec(memory_space=pltpu.HBM)
+    return pl.pallas_call(
+        put_out,
+        name="put_out",
+        out_shape=(
+            jax.ShapeDtypeStruct((2, 128, 512), F32),
+            jax.ShapeDtypeStruct((2, 64, 512), F32),
+        ),
+        in_specs=[vmem, vmem],
+        out_specs=(hbm, hbm),
+        scratch_shapes=[pltpu.SemaphoreType.DMA((2,))],
+        compiler_params=pltpu.CompilerParams(vmem_limit_bytes=4 << 20),
+    )(*results)
 
 
 def solution(mesh):

time: 63.1 us -> 62.7 us (level)
  local copies, waits for them, and re-layouts: 1.5 us -> 0 us
  Pallas kernels: 60.9 us -> 61.8 us
    unnamed x2 -> x0, local copies, waits for them, and re-layouts: 1.5 us -> none
    pallas_call x0 -> x1, Pallas kernels: none -> 0.89 us  [body(): pl.pallas_call(put_out, name='put_out', out_shape=(jax.ShapeDtypeStruct((...]
where the time goes in v8:
time: 62.7 us; the launch traced here: 62.6 us
  Pallas kernels  61.8 us (99%)
  between operations  0.8 us (1%)
    pallas_call x1, Pallas kernels, body(): pl.pallas_call(kernel, name='chain', out_shape=(pltpu.VMEM((2, 128, 512),...  60.9 us

profile of v8, /device:TPU:33, one launch (start us, length us, event | category | flops | bytes accessed | tf_op | source)
XLA Modules:
  0.0 62.6 jit_solution(17496846920849267503)
XLA Ops:
  0.6 60.9 %chain.1 = (f32[2,128,512]{2,1,0:T(8,128)S(1)}, f32[2,64,512]{2,1,0:T(8,128)S(1)}) custom-call(s32[2,4]{1,0:T(2,128)} %blocks_hbm.1, s32[2,4]{1,0:T(2,128)} %mask_hbm.1, f32[2,512,512]{2,1,0:T(8,128)} %inv_hbm.1, f32[2,64,512]{2,1,0:T(8,128)} %fac_hbm.1), custom_call_target="tpu_custom_call" | custom-call | tf_op jit(solution)/shard_map/chain/pallas_call | solution.py:625
  61.5 0.9 %put_out.1 = (f32[2,128,512]{2,1,0:T(8,128)}, f32[2,64,512]{2,1,0:T(8,128)}) custom-call(f32[2,128,512]{2,1,0:T(8,128)S(1)} %get-tuple-element.4.cov, f32[2,64,512]{2,1,0:T(8,128)S(1)} %get-tuple-element.5.off), custom_call_target="tpu_custom_call" | custom-call | tf_op jit(solution)/shard_map/put_out/pallas_call | solution.py:667

commit v9 on v8

--- a/solution.py
+++ b/solution.py
@@ -427,8 +427,6 @@
     ring_send(ya, ID_YA, y, y_at, constant_part)
 
     yl_mates = direct(yl, ID_YL, y, y_at, link_part)
-    z_next(fg, ID_ZF, 1, 0)
-    z_next(fg, ID_ZF, 0, 0, cond=is_b)
     ya_mates = direct(ya, ID_YA, y, y_at, constant_part)
     done(yl_mates)
     done(ya_mates)
@@ -460,7 +458,8 @@
     low = mm(split(yl[1]), split(yl[0]))
     xl[x] = mm(split(high), split(low))
     ring_send(xl, ID_XL, x, x_at, link_part)
-    z_next(fg, ID_ZF, 1, 1)
+    z_next(fg, ID_ZF, 1, 0)
+    z_next(fg, ID_ZF, 0, 0, cond=is_b)
 
     @pl.when(y == 0)
     def _():
@@ -479,7 +478,6 @@
     xa[x] = term(ya, across, sm[...])
     ring_send(xa, ID_XA, x, x_at, constant_part)
 
-    z_next(fg, ID_ZF, 0, 1, cond=is_b)
     exclusive_links(yl, y, el.at[1])
     exclusive_constants(yl, ya, y, ea.at[1])
     xl_mates = direct(xl, ID_XL, x, x_at, link_part)
@@ -492,6 +490,8 @@
     ea[0] = sandwich(lp[1], ea[1], base[1])
     el[0] = mm(split(el[1]), split(lp[1]))
 
+    z_next(fg, ID_ZF, 1, 1)
+    z_next(fg, ID_ZF, 0, 1, cond=is_b)
     xa_mates = direct(xa, ID_XA, x, x_at, constant_part)
     done(xl_mates + opposite(xl, ID_XL, x, link_part))
     sends_half = both(later, edge)
@@ -559,6 +559,14 @@
             zh(j, 2).start()
 
     outputs(0)
+    for sends, one in started:
+        if sends is None:
+            one.wait_send()
+        else:
+
+            @pl.when(sends)
+            def _():
+                one().wait_send()
 
     @pl.when(both(h == 0, jnp.logical_not(edge)))
     def _():
@@ -579,15 +587,6 @@
 
     for p in (0, 1):
         off[p] = off[p] * (-mask[p, r].astype(F32))
-
-    for sends, one in started:
-        if sends is None:
-            one.wait_send()
-        else:
-
-            @pl.when(sends)
-            def _():
-                one().wait_send()
 
     @pl.when(sends_half)
     def _():

time: 62.7 us -> 62.5 us (level)
  no operation moved by 1% of the time
where the time goes in v9:
time: 62.5 us; the launch traced here: 62.4 us
  Pallas kernels  61.6 us (99%)
  between operations  0.8 us (1%)
    pallas_call x1, Pallas kernels, body(): pl.pallas_call(kernel, name='chain', out_shape=(pltpu.VMEM((2, 128, 512),...  60.7 us

profile of v9, /device:TPU:33, one launch (start us, length us, event | category | flops | bytes accessed | tf_op | source)
XLA Modules:
  0.0 62.4 jit_solution(3519804504121145466)
XLA Ops:
  0.6 60.7 %chain.1 = (f32[2,128,512]{2,1,0:T(8,128)S(1)}, f32[2,64,512]{2,1,0:T(8,128)S(1)}) custom-call(s32[2,4]{1,0:T(2,128)} %blocks_hbm.1, s32[2,4]{1,0:T(2,128)} %mask_hbm.1, f32[2,512,512]{2,1,0:T(8,128)} %inv_hbm.1, f32[2,64,512]{2,1,0:T(8,128)} %fac_hbm.1), custom_call_target="tpu_custom_call" | custom-call | tf_op jit(solution)/shard_map/chain/pallas_call | solution.py:624
  61.4 0.9 %put_out.1 = (f32[2,128,512]{2,1,0:T(8,128)}, f32[2,64,512]{2,1,0:T(8,128)}) custom-call(f32[2,128,512]{2,1,0:T(8,128)S(1)} %get-tuple-element.4.cov, f32[2,64,512]{2,1,0:T(8,128)S(1)} %get-tuple-element.5.off), custom_call_target="tpu_custom_call" | custom-call | tf_op jit(solution)/shard_map/put_out/pallas_call | solution.py:666

commit v10 on v9

--- a/solution.py
+++ b/solution.py
@@ -157,7 +157,9 @@
         ih, il = split(inv[p])
         inv_h[p] = ih
         inv_l[p] = il
-        fg[p, pl.ds(r * 64, 64), :] = mm(split(fac[p] * keep(p)), (ih, il))
+        fh, fl = split(fac[p] * keep(p))
+        fg[p, pl.ds(r * 64, 64), :256] = mm((fh, fl), (ih[:, :256], il[:, :256]))
+        fg[p, pl.ds(r * 64, 64), 256:] = mm((fh[:, 256:], fl[:, 256:]), (ih[256:, 256:], il[256:, 256:]))
 
     def local_link(p, choose):
         fh, fl = split(fg[p, pl.ds(r * 64, 64), :])
@@ -289,15 +291,16 @@
     for p in (0, 1):
         mine = inv[p, :, pl.ds(pl.multiple_of(r * 128, 128), 128)]
         cov[p] = mm(split(mine.T), (inv_h[p], inv_l[p]))
+
+    @pl.when(relay_in)
+    def _():
+        relay().wait_recv()
+
+    @pl.when(waits_long)
+    def _():
+        local_base(0, chooser(idx_in[...]))
+
     every(2)
-
-    @pl.when(relay_in)
-    def _():
-        relay().wait_recv()
-
-    @pl.when(waits_long)
-    def _():
-        local_base(0, chooser(idx_in[...]))
 
     @pl.when(is_a)
     def _():

time: 62.5 us -> 62.6 us (level)
  no operation moved by 1% of the time
where the time goes in v10:
time: 62.6 us; the launch traced here: 62.4 us
  Pallas kernels  61.6 us (98%)
  between operations  0.8 us (1%)
    pallas_call x1, Pallas kernels, body(): pl.pallas_call(kernel, name='chain', out_shape=(pltpu.VMEM((2, 128, 512),...  60.8 us

profile of v10, /device:TPU:33, one launch (start us, length us, event | category | flops | bytes accessed | tf_op | source)
XLA Modules:
  0.0 62.4 jit_solution(12874156351218971442)
XLA Ops:
  0.6 60.8 %chain.1 = (f32[2,128,512]{2,1,0:T(8,128)S(1)}, f32[2,64,512]{2,1,0:T(8,128)S(1)}) custom-call(s32[2,4]{1,0:T(2,128)} %blocks_hbm.1, s32[2,4]{1,0:T(2,128)} %mask_hbm.1, f32[2,512,512]{2,1,0:T(8,128)} %inv_hbm.1, f32[2,64,512]{2,1,0:T(8,128)} %fac_hbm.1), custom_call_target="tpu_custom_call" | custom-call | tf_op jit(solution)/shard_map/chain/pallas_call | solution.py:627
  61.4 0.9 %put_out.1 = (f32[2,128,512]{2,1,0:T(8,128)}, f32[2,64,512]{2,1,0:T(8,128)}) custom-call(f32[2,128,512]{2,1,0:T(8,128)S(1)} %get-tuple-element.4.cov, f32[2,64,512]{2,1,0:T(8,128)S(1)} %get-tuple-element.5.off), custom_call_target="tpu_custom_call" | custom-call | tf_op jit(solution)/shard_map/put_out/pallas_call | solution.py:669

commit v11 on v10

--- a/solution.py
+++ b/solution.py
@@ -49,7 +49,7 @@
 def kernel(
     blocks_hbm, mask_hbm, inv_hbm, fac_hbm, cov, off,
     blocks, mask, inv, fac, local, idx_out, idx_in, inv_h, inv_l, lp, fg, base, cl, ca, yl, ya, xl, xa,
-    el, ea, ph, th, pb, rb, sm, gg, kk, ss, rs,
+    el, ea, ph, th, pb, rb, sm, gg, gh, gl, kh, kl, cz, ss, rs,
 ):
     h, x, y, c = (lax.axis_index(a) for a in SEG)
     r = lax.axis_index("row")
@@ -300,13 +300,22 @@
     def _():
         local_base(0, chooser(idx_in[...]))
 
+    def choose_rows(cond, lo, n):
+        @pl.when(both(is_a, cond))
+        def _():
+            fh, fl = split(fg[0, lo : lo + n, :])
+            lp[0, lo : lo + n, :] = dot(fh, cz[...]) + dot(fl, cz[...])
+
+    @pl.when(is_a)
+    def _():
+        cz[...] = chooser(idx_in[...])
+
+    choose_rows(r == 0, 0, 192)
+    choose_rows(r == 3, 64, 192)
+    choose_rows(jnp.logical_not(edge), 0, 256)
     every(2)
-
-    @pl.when(is_a)
-    def _():
-        fh, fl = split(fg[0])
-        choose = chooser(idx_in[...])
-        lp[0] = dot(fh, choose) + dot(fl, choose)
+    choose_rows(r == 0, 192, 64)
+    choose_rows(r == 3, 0, 64)
 
     z_send(fg, ID_ZF, 1, 0)
     z_send(fg, ID_ZF, 0, 0, cond=is_b)
@@ -517,8 +526,10 @@
             link = mm(entry, split(el[p]))
             pb[...] = link.T
             gg[p] = mm(split(link), split(fg[p]))
-            kk[p * 192 : p * 192 + 128, :] = gg[p, :, pl.ds(pl.multiple_of(r * 128, 128), 128)].T
-            kk[p * 192 + 128 : p * 192 + 192, :] = pb[pl.ds(r * 64, 64), :]
+            gh[p], gl[p] = split(gg[p])
+            own = gg[p, :, pl.ds(pl.multiple_of(r * 128, 128), 128)].T
+            at = slice(p * 192, p * 192 + 192)
+            kh[at, :], kl[at, :] = split(jnp.concatenate([own, pb[pl.ds(r * 64, 64), :]], 0))
 
     done(opposite(xa, ID_XA, x, constant_part))
 
@@ -581,10 +592,10 @@
     def _():
         for j in (0, 1, 2):
             zh(j, 2).wait_recv()
-        left = split(mm(split(kk[...]), split(whole(ph[...]))))
+        left = split(mm((kh[...], kl[...]), split(whole(ph[...]))))
         for p in (0, 1):
             at = slice(p * 192, p * 192 + 192)
-            out = mm((left[0][at], left[1][at]), split(gg[p]))
+            out = mm((left[0][at], left[1][at]), (gh[p], gl[p]))
             cov[p] += out[:128]
             off[p] += out[128:]
 
@@ -657,7 +668,11 @@
             sq(4),
             pltpu.VMEM((256, 256), F32),
             pltpu.VMEM((2, 256, 512), F32),
-            pltpu.VMEM((384, 256), F32),
+            pltpu.VMEM((2, 256, 512), BF16),
+            pltpu.VMEM((2, 256, 512), BF16),
+            pltpu.VMEM((384, 256), BF16),
+            pltpu.VMEM((384, 256), BF16),
+            pltpu.VMEM((512, 256), BF16),
             pltpu.SemaphoreType.DMA((N_IDS,)),
             pltpu.SemaphoreType.DMA((N_IDS,)),
         ],

time: 62.6 us -> 62.5 us (level)
  no operation moved by 1% of the time
where the time goes in v11:
time: 62.5 us; the launch traced here: 62.3 us
  Pallas kernels  61.5 us (98%)
  between operations  0.8 us (1%)
    pallas_call x1, Pallas kernels, body(): pl.pallas_call(kernel, name='chain', out_shape=(pltpu.VMEM((2, 128, 512),...  60.6 us

profile of v11, /device:TPU:33, one launch (start us, length us, event | category | flops | bytes accessed | tf_op | source)
XLA Modules:
  0.0 62.3 jit_solution(6310535963026651833)
XLA Ops:
  0.6 60.6 %chain.1 = (f32[2,128,512]{2,1,0:T(8,128)S(1)}, f32[2,64,512]{2,1,0:T(8,128)S(1)}) custom-call(s32[2,4]{1,0:T(2,128)} %blocks_hbm.1, s32[2,4]{1,0:T(2,128)} %mask_hbm.1, f32[2,512,512]{2,1,0:T(8,128)} %inv_hbm.1, f32[2,64,512]{2,1,0:T(8,128)} %fac_hbm.1), custom_call_target="tpu_custom_call" | custom-call | tf_op jit(solution)/shard_map/chain/pallas_call | solution.py:638
  61.3 0.9 %put_out.1 = (f32[2,128,512]{2,1,0:T(8,128)}, f32[2,64,512]{2,1,0:T(8,128)}) custom-call(f32[2,128,512]{2,1,0:T(8,128)S(1)} %get-tuple-element.4.cov, f32[2,64,512]{2,1,0:T(8,128)S(1)} %get-tuple-element.5.off), custom_call_target="tpu_custom_call" | custom-call | tf_op jit(solution)/shard_map/put_out/pallas_call | solution.py:684

commit v12 on v10

--- a/solution.py
+++ b/solution.py
@@ -308,8 +308,6 @@
         choose = chooser(idx_in[...])
         lp[0] = dot(fh, choose) + dot(fl, choose)
 
-    z_send(fg, ID_ZF, 1, 0)
-    z_send(fg, ID_ZF, 0, 0, cond=is_b)
 
     link_0 = split(lp[0])
     cl[c] = mm(split(lp[1]), link_0)
@@ -428,6 +426,8 @@
     ca_copy.wait_recv()
     ya[y] = sandwich(cl[0], ca[1], ca[0])
     ring_send(ya, ID_YA, y, y_at, constant_part)
+    z_send(fg, ID_ZF, 1, 0)
+    z_send(fg, ID_ZF, 0, 0, cond=is_b)
 
     yl_mates = direct(yl, ID_YL, y, y_at, link_part)
     ya_mates = direct(ya, ID_YA, y, y_at, constant_part)
@@ -608,10 +608,11 @@
 
 
 def put_out(cov, off, cov_out, off_out, sems):
-    copies = (
-        pltpu.make_async_copy(cov, cov_out, sems.at[0]),
-        pltpu.make_async_copy(off, off_out, sems.at[1]),
-    )
+    copies = [
+        pltpu.make_async_copy(src.at[p], dst.at[p], sems.at[2 * i + p])
+        for i, (src, dst) in enumerate(((cov, cov_out), (off, off_out)))
+        for p in (0, 1)
+    ]
     for one in copies:
         one.start()
     for one in copies:
@@ -675,7 +676,7 @@
         ),
         in_specs=[vmem, vmem],
         out_specs=(hbm, hbm),
-        scratch_shapes=[pltpu.SemaphoreType.DMA((2,))],
+        scratch_shapes=[pltpu.SemaphoreType.DMA((4,))],
         compiler_params=pltpu.CompilerParams(vmem_limit_bytes=4 << 20),
     )(*results)
 

time: 62.6 us -> 61.5 us (0.982)
  Pallas kernels: 61.6 us -> 60 us
    pallas_call x1, Pallas kernels: 60.8 us -> 59.1 us  [body(): pl.pallas_call(kernel, name='chain', out_shape=(pltpu.VMEM((2, 128, 512),...]
where the time goes in v12:
time: 61.5 us; the launch traced here: 60.8 us
  Pallas kernels  60 us (98%)
  between operations  0.8 us (1%)
    pallas_call x1, Pallas kernels, body(): pl.pallas_call(kernel, name='chain', out_shape=(pltpu.VMEM((2, 128, 512),...  59.1 us

profile of v12, /device:TPU:33, one launch (start us, length us, event | category | flops | bytes accessed | tf_op | source)
XLA Modules:
  0.0 60.8 jit_solution(11669184554764864198)
XLA Ops:
  0.6 59.1 %chain.1 = (f32[2,128,512]{2,1,0:T(8,128)S(1)}, f32[2,64,512]{2,1,0:T(8,128)S(1)}) custom-call(s32[2,4]{1,0:T(2,128)} %blocks_hbm.1, s32[2,4]{1,0:T(2,128)} %mask_hbm.1, f32[2,512,512]{2,1,0:T(8,128)} %inv_hbm.1, f32[2,64,512]{2,1,0:T(8,128)} %fac_hbm.1), custom_call_target="tpu_custom_call" | custom-call | tf_op jit(solution)/shard_map/chain/pallas_call | solution.py:628
  59.7 0.9 %put_out.1 = (f32[2,128,512]{2,1,0:T(8,128)}, f32[2,64,512]{2,1,0:T(8,128)}) custom-call(f32[2,128,512]{2,1,0:T(8,128)S(1)} %get-tuple-element.4.cov, f32[2,64,512]{2,1,0:T(8,128)S(1)} %get-tuple-element.5.off), custom_call_target="tpu_custom_call" | custom-call | tf_op jit(solution)/shard_map/put_out/pallas_call | solution.py:670

commit v13 on v12

--- a/solution.py
+++ b/solution.py
@@ -426,11 +426,11 @@
     ca_copy.wait_recv()
     ya[y] = sandwich(cl[0], ca[1], ca[0])
     ring_send(ya, ID_YA, y, y_at, constant_part)
+
+    yl_mates = direct(yl, ID_YL, y, y_at, link_part)
+    ya_mates = direct(ya, ID_YA, y, y_at, constant_part)
     z_send(fg, ID_ZF, 1, 0)
     z_send(fg, ID_ZF, 0, 0, cond=is_b)
-
-    yl_mates = direct(yl, ID_YL, y, y_at, link_part)
-    ya_mates = direct(ya, ID_YA, y, y_at, constant_part)
     done(yl_mates)
     done(ya_mates)
 
@@ -461,8 +461,6 @@
     low = mm(split(yl[1]), split(yl[0]))
     xl[x] = mm(split(high), split(low))
     ring_send(xl, ID_XL, x, x_at, link_part)
-    z_next(fg, ID_ZF, 1, 0)
-    z_next(fg, ID_ZF, 0, 0, cond=is_b)
 
     @pl.when(y == 0)
     def _():
@@ -484,6 +482,8 @@
     exclusive_links(yl, y, el.at[1])
     exclusive_constants(yl, ya, y, ea.at[1])
     xl_mates = direct(xl, ID_XL, x, x_at, link_part)
+    z_next(fg, ID_ZF, 1, 0)
+    z_next(fg, ID_ZF, 0, 0, cond=is_b)
 
     @pl.when(c == 0)
     def _():

time: 61.5 us -> 65.8 us (1.070)
  the two profiles are of different devices: /device:TPU:33 before, /device:TPU:43 now
where the time goes in v13:
time: 65.8 us; the launch traced here: 65.7 us
  Pallas kernels  64.9 us (99%)
  between operations  0.8 us (1%)
    pallas_call x1, Pallas kernels, body(): pl.pallas_call(kernel, name='chain', out_shape=(pltpu.VMEM((2, 128, 512),...  64 us

profile of v13, /device:TPU:43, one launch (start us, length us, event | category | flops | bytes accessed | tf_op | source)
XLA Modules:
  0.0 65.7 jit_solution(4384555671682310583)
XLA Ops:
  0.6 64.0 %chain.1 = (f32[2,128,512]{2,1,0:T(8,128)S(1)}, f32[2,64,512]{2,1,0:T(8,128)S(1)}) custom-call(s32[2,4]{1,0:T(2,128)} %blocks_hbm.1, s32[2,4]{1,0:T(2,128)} %mask_hbm.1, f32[2,512,512]{2,1,0:T(8,128)} %inv_hbm.1, f32[2,64,512]{2,1,0:T(8,128)} %fac_hbm.1), custom_call_target="tpu_custom_call" | custom-call | tf_op jit(solution)/shard_map/chain/pallas_call | solution.py:628
  64.6 0.9 %put_out.1 = (f32[2,128,512]{2,1,0:T(8,128)}, f32[2,64,512]{2,1,0:T(8,128)}) custom-call(f32[2,128,512]{2,1,0:T(8,128)S(1)} %get-tuple-element.4.cov, f32[2,64,512]{2,1,0:T(8,128)S(1)} %get-tuple-element.5.off), custom_call_target="tpu_custom_call" | custom-call | tf_op jit(solution)/shard_map/put_out/pallas_call | solution.py:670
